TPU v7x, 32 devices: a whole 2x2x4 slice. The times are simulated.
32 devices in a mesh: section: 2 (over x), dp: 16 (over z, y, core).
Axes of the slice: x: 2, y: 2, z: 4, core: 2. Of those that a mesh axis runs over, the one named last changes fastest.
Arguments:
- block_input: float32 [2048, 1024], P('dp'), may hold values from -6 to 6
- cotangent: float32 [2048, 1024], P('dp'), may hold values from -6 to 6
- marks: int32 [2048], P('dp'), may hold values 0 or 1
- w_in: bfloat16 [2, 1024, 4096], P('section', 'dp'), may hold values from -0.1875 to 0.1875
- w_out: bfloat16 [2, 1024, 1024], P('section', 'dp'), may hold values from -0.1875 to 0.1875
- w_up: bfloat16 [2, 1024, 5632], P('section', 'dp'), may hold values from -0.1875 to 0.1875
- w_down: bfloat16 [2, 1024, 2816], P('section', 'dp'), may hold values from -0.109375 to 0.109375
- gate_weights: bfloat16 [2, 1024, 16], P('section'), may hold values from -0.1875 to 0.1875
- norm_gains: float32 [2, 2, 1024], P('section'), may hold values from 0.5 to 1.5
- conv_weights: float32 [2, 4, 3072], P('section'), may hold values from -3 to 3
- decay_log: float32 [2, 8], P('section'), may hold values from -4 to 1
- decay_bias: float32 [2, 8], P('section'), may hold values from -4 to 0
- out_gain: float32 [2, 128], P('section'), may hold values from 0.5 to 1.5
Outputs:
- layer_outputs: float32 [2, 2048, 1024], P('section', 'dp')
- input_grads: float32 [2, 2048, 1024], P('section', 'dp')
- grad_w_in: float32 [2, 1024, 4096], P('section', 'dp')
- grad_w_out: float32 [2, 1024, 1024], P('section', 'dp')
- grad_w_up: float32 [2, 1024, 5632], P('section', 'dp')
- grad_w_down: float32 [2, 1024, 2816], P('section', 'dp')
- grad_gate_weights: float32 [2, 1024, 16], P('section')
- grad_norm_gains: float32 [2, 2, 1024], P('section')
- grad_conv_weights: float32 [2, 4, 3072], P('section')
- grad_decay_log: float32 [2, 8], P('section')
- grad_decay_bias: float32 [2, 8], P('section')
- grad_out_gain: float32 [2, 128], P('section')
Inputs may be any that keep to these rules, and one draw needn't show every extreme that they name: A 1 marks the first token of a sequence; the first of every 128 rows begins a sequence whatever its mark.
All inputs are finite; a program needn't handle non-finite values. No bound on the sum of `marks` on one device may be relied on, other than what follows from the above.
Results may differ from a plain program's by a relative error of at most 0.01575.
Values may be sent and summed in bfloat16 or wider, within the bound.
A program may use at most 256 MiB of HBM per device.

v0:
```python
import jax
import jax.numpy as jnp
from jax import lax
from jax.sharding import PartitionSpec as P

D = 1024
FF = 2816
HEADS = 8
HEAD_DIM = 128
CONV = 4
GROUP = 64


epsilon = 1e-06
highest = lax.Precision.HIGHEST


def passed_along(value, axis, steps):
    count = lax.axis_size(axis)
    initial, last = (max(0, -steps), min(count, count - steps))
    return lax.ppermute(value, axis, [(source, source + steps) for source in range(initial, last)])


def dot_rows(left, right):
    return lax.dot_general(
        left, right, (((1,), (1,)), ((), ())), preferred_element_type=jnp.float32
    )


def dot_cols(left, right):
    return lax.dot_general(
        left, right, (((0,), (0,)), ((), ())), preferred_element_type=jnp.float32
    )


def rms_scale(values, gain):
    return values * lax.rsqrt(jnp.mean(values * values, axis=-1, keepdims=True) + epsilon) * gain


def segment_ids(marks_block):
    position = jnp.arange(marks_block.shape[0])
    starts = jnp.logical_or(marks_block > 0, position == 0).astype(jnp.int32)
    return jnp.cumsum(starts)


def short_conv(columns, kernel, segment):
    row_count, width = columns.shape
    total = columns * kernel[CONV - 1]
    for offset in range(1, CONV):
        shifted = jnp.concatenate(
            [jnp.zeros((offset, width), columns.dtype), columns[: row_count - offset]], axis=0
        )
        same = jnp.concatenate(
            [jnp.zeros((offset,), jnp.bool_), segment[offset:] == segment[: row_count - offset]]
        )
        total = total + jnp.where(same[:, None], shifted, 0.0) * kernel[CONV - 1 - offset]
    return jax.nn.silu(total)


def delta_rule(queries, key_rows, value_rows, beta_rows, log_decay, segment):
    row_count = queries.shape[0]
    blocks = row_count // GROUP

    def to_blocks(array):
        shaped = array.reshape((blocks, GROUP, HEADS) + array.shape[2:])
        return jnp.moveaxis(shaped, 2, 1)

    seg_blocks = segment.reshape(blocks, GROUP)
    before = jnp.concatenate([jnp.full((1,), -1, jnp.int32), seg_blocks[:-1, GROUP - 1]])
    index_a = jnp.arange(GROUP)[:, None]
    index_b = jnp.arange(GROUP)[None, :]
    lower = index_a >= index_b
    strict = index_a > index_b
    identity = jnp.eye(GROUP, dtype=jnp.float32)

    def step_block(state, inputs):
        query_b, key_b, value_b, beta_b, decay_b, seg_b, prior = inputs
        cumul = jnp.cumsum(decay_b, axis=1)
        within = jnp.logical_and(seg_b[:, None] == seg_b[None, :], lower)
        spread = cumul[:, :, None] - cumul[:, None, :]
        weights_in = jnp.where(within[None], jnp.exp(jnp.minimum(spread, 0.0)), 0.0)
        carried = jnp.where((seg_b == prior)[None, :], jnp.exp(cumul), 0.0)
        key_key = jnp.einsum("hid,hjd->hij", key_b, key_b, precision=highest)
        left_side = (
            identity + jnp.where(strict[None], weights_in, 0.0) * key_key * beta_b[:, :, None]
        )
        state_keys = jnp.einsum("hid,hed->hie", key_b, state, precision=highest)
        right_side = beta_b[:, :, None] * (value_b - carried[:, :, None] * state_keys)
        pseudo = lax.linalg.triangular_solve(
            left_side, right_side, left_side=True, lower=True, unit_diagonal=True
        )
        query_key = jnp.einsum("hid,hjd->hij", query_b, key_b, precision=highest)
        state_query = jnp.einsum("hid,hed->hie", query_b, state, precision=highest)
        output = carried[:, :, None] * state_query + jnp.einsum(
            "hij,hje->hie", query_key * weights_in, pseudo, precision=highest
        )
        tail = weights_in[:, GROUP - 1, :]
        state = carried[:, GROUP - 1][:, None, None] * state + jnp.einsum(
            "hje,hjd->hed", pseudo * tail[:, :, None], key_b, precision=highest
        )
        return (state, output)

    start_state = jnp.zeros((HEADS, HEAD_DIM, HEAD_DIM), jnp.float32)
    inputs = (
        to_blocks(queries),
        to_blocks(key_rows),
        to_blocks(value_rows),
        to_blocks(beta_rows),
        to_blocks(log_decay),
        seg_blocks,
        before,
    )
    _, outputs = lax.scan(step_block, start_state, inputs)
    return jnp.moveaxis(outputs, 1, 2).reshape(row_count, HEADS, HEAD_DIM)


def mixer_core(proj, gate_pre, kernel, decay_log, decay_bias, out_gain, segment):
    row_count = proj.shape[0]
    mixed_in = short_conv(proj[:, : 3 * D], kernel, segment)
    heads_shape = (row_count, HEADS, HEAD_DIM)
    query_raw = mixed_in[:, :D].reshape(heads_shape)
    key_raw = mixed_in[:, D : 2 * D].reshape(heads_shape)
    value_rows = mixed_in[:, 2 * D :].reshape(heads_shape)
    queries = (
        query_raw
        * lax.rsqrt(jnp.sum(query_raw * query_raw, axis=-1, keepdims=True) + epsilon)
        * HEAD_DIM ** (-0.5)
    )
    key_rows = key_raw * lax.rsqrt(jnp.sum(key_raw * key_raw, axis=-1, keepdims=True) + epsilon)
    beta_rows = jax.nn.sigmoid(gate_pre[:, HEADS:])
    log_decay = -jnp.exp(decay_log) * jax.nn.softplus(gate_pre[:, :HEADS] + decay_bias)
    delta_out = delta_rule(queries, key_rows, value_rows, beta_rows, log_decay, segment)
    scaled = (
        delta_out
        * lax.rsqrt(jnp.mean(delta_out * delta_out, axis=-1, keepdims=True) + epsilon)
        * out_gain
    )
    gate_part = proj[:, 3 * D :].reshape(heads_shape)
    return (scaled * jax.nn.silu(gate_part)).reshape(row_count, D)


def swiglu(upgate):
    return jax.nn.silu(upgate[:, :FF]) * upgate[:, FF:]


def layer_forward(
    w_in,
    w_out,
    w_up,
    w_down,
    gate_weights,
    norm_gains,
    kernel,
    decay_log,
    decay_bias,
    out_gain,
    block,
    marks_block,
):
    segment = segment_ids(marks_block)
    normed_a = rms_scale(block, norm_gains[0]).astype(jnp.bfloat16)
    proj = jnp.dot(normed_a, w_in, preferred_element_type=jnp.float32)
    gate_pre = jnp.dot(normed_a, gate_weights, preferred_element_type=jnp.float32)
    mixer = mixer_core(proj, gate_pre, kernel, decay_log, decay_bias, out_gain, segment).astype(
        jnp.bfloat16
    )
    middle = block + jnp.dot(mixer, w_out, preferred_element_type=jnp.float32)
    normed_f = rms_scale(middle, norm_gains[1]).astype(jnp.bfloat16)
    upgate = jnp.dot(normed_f, w_up, preferred_element_type=jnp.float32)
    hidden = swiglu(upgate).astype(jnp.bfloat16)
    result = middle + dot_rows(hidden, w_down)
    return (result, (normed_a, proj, gate_pre, mixer, middle, normed_f, upgate, hidden))


def layer_backward(
    w_in,
    w_out,
    w_up,
    w_down,
    gate_weights,
    norm_gains,
    kernel,
    decay_log,
    decay_bias,
    out_gain,
    block,
    marks_block,
    saved,
    grad_out,
):
    segment = segment_ids(marks_block)
    normed_a, proj, gate_pre, mixer, middle, normed_f, upgate, hidden = saved
    g_bf = grad_out.astype(jnp.bfloat16)
    d_hidden = jnp.dot(g_bf, w_down, preferred_element_type=jnp.float32)
    _, swiglu_back = jax.vjp(swiglu, upgate)
    d_upgate = swiglu_back(d_hidden)[0].astype(jnp.bfloat16)
    d_normed_f = dot_rows(d_upgate, w_up)
    _, norm_back_f = jax.vjp(rms_scale, middle, norm_gains[1])
    d_middle, gain_f = norm_back_f(d_normed_f)
    d_middle = d_middle + grad_out
    dm_bf = d_middle.astype(jnp.bfloat16)
    d_mixer = dot_rows(dm_bf, w_out)

    def core_of(proj_in, gate_in, kernel_in, log_in, bias_in, gain_in):
        return mixer_core(proj_in, gate_in, kernel_in, log_in, bias_in, gain_in, segment)

    _, core_back = jax.vjp(core_of, proj, gate_pre, kernel, decay_log, decay_bias, out_gain)
    d_proj, d_gate_pre, d_kernel, d_log, d_bias, d_gain = core_back(d_mixer)
    d_proj = d_proj.astype(jnp.bfloat16)
    d_gate_pre = d_gate_pre.astype(jnp.bfloat16)
    d_normed_a = dot_rows(d_proj, w_in) + dot_rows(d_gate_pre, gate_weights)
    _, norm_back_a = jax.vjp(rms_scale, block, norm_gains[0])
    d_block, gain_a = norm_back_a(d_normed_a)
    d_block = d_block + d_middle
    small = (
        dot_cols(normed_a, d_gate_pre),
        jnp.stack([gain_a, gain_f]),
        d_kernel,
        d_log,
        d_bias,
        d_gain,
    )
    factors = (normed_a, d_proj, mixer, dm_bf, normed_f, d_upgate, g_bf, hidden)
    return (d_block, small, factors)


def mixer_terms(factors):
    normed_a, d_proj, mixer, dm_bf = factors[:4]
    return jnp.concatenate([dot_cols(normed_a, d_proj), dot_cols(mixer, dm_bf)], axis=1)


def ffn_terms(factors):
    normed_f, d_upgate, g_bf, hidden = factors[4:]
    return jnp.concatenate([dot_cols(normed_f, d_upgate), dot_cols(g_bf, hidden)], axis=1)


def active_or_quiet(predicate, thunk):
    return lax.cond(predicate, thunk, lambda: jax.tree.map(jnp.zeros_like, thunk()))


def local(
    block_input,
    cotangent,
    marks,
    w_in,
    w_out,
    w_up,
    w_down,
    gate_weights,
    norm_gains,
    conv_weights,
    decay_log,
    decay_bias,
    out_gain,
):
    section_index = lax.axis_index("section")
    first_section = section_index == 0
    later_section = jnp.logical_not(first_section)
    small_params = (
        gate_weights[0],
        norm_gains[0],
        conv_weights[0],
        decay_log[0],
        decay_bias[0],
        out_gain[0],
    )
    gathered = (
        lax.all_gather(w_in[0], "dp", axis=0, tiled=True),
        lax.all_gather(w_out[0], "dp", axis=0, tiled=True),
        lax.all_gather(w_up[0], "dp", axis=0, tiled=True),
        lax.all_gather(w_down[0], "dp", axis=0, tiled=True),
    )

    def run_forward(source):
        return layer_forward(*gathered, *small_params, source, marks)

    first_out, first_saved = active_or_quiet(first_section, lambda: run_forward(block_input))
    arrived = passed_along(first_out, "section", 1)
    second_out, second_saved = active_or_quiet(later_section, lambda: run_forward(arrived))
    layer_out = first_out + second_out
    saved = jax.tree.map(jnp.add, first_saved, second_saved)
    source = jnp.where(first_section, block_input, arrived)
    back_weights = (
        lax.all_gather(w_in[0], "dp", axis=0, tiled=True),
        lax.all_gather(w_out[0], "dp", axis=0, tiled=True),
        lax.all_gather(w_up[0], "dp", axis=0, tiled=True),
        lax.all_gather(w_down[0], "dp", axis=0, tiled=True),
    )

    def run_backward(grad_out):
        return layer_backward(*back_weights, *small_params, source, marks, saved, grad_out)

    late_grad, late_small, late_factors = active_or_quiet(
        later_section, lambda: run_backward(cotangent)
    )
    returned = passed_along(late_grad.astype(jnp.bfloat16), "section", -1).astype(late_grad.dtype)
    early_grad, early_small, early_factors = active_or_quiet(
        first_section, lambda: run_backward(returned)
    )
    input_grad = late_grad + early_grad
    factors = jax.tree.map(jnp.add, late_factors, early_factors)
    small_local = jax.tree.map(jnp.add, late_small, early_small)
    ffn_part = lax.psum_scatter(ffn_terms(factors), "dp", scatter_dimension=0, tiled=True)
    mixer_part = lax.psum_scatter(mixer_terms(factors), "dp", scatter_dimension=0, tiled=True)
    terms = jnp.concatenate([mixer_part, ffn_part], axis=1)
    small_sums = lax.psum(small_local, "dp")
    grad_gate, grad_gains, grad_conv, grad_log, grad_bias, grad_gain = small_sums
    return (
        layer_out[None],
        input_grad[None],
        terms[:, : 4 * D][None],
        terms[:, 4 * D : 5 * D][None],
        terms[:, 5 * D : 5 * D + 2 * FF][None],
        terms[:, 5 * D + 2 * FF :][None],
        grad_gate[None],
        grad_gains[None],
        grad_conv[None],
        grad_log[None],
        grad_bias[None],
        grad_gain[None],
    )


def solution(mesh):
    return jax.shard_map(
        local,
        mesh=mesh,
        in_specs=(
            P("dp", None),
            P("dp", None),
            P("dp"),
            P("section", "dp", None),
            P("section", "dp", None),
            P("section", "dp", None),
            P("section", "dp", None),
            P("section", None, None),
            P("section", None, None),
            P("section", None, None),
            P("section", None),
            P("section", None),
            P("section", None),
        ),
        out_specs=(
            P("section", "dp", None),
            P("section", "dp", None),
            P("section", "dp", None),
            P("section", "dp", None),
            P("section", "dp", None),
            P("section", "dp", None),
            P("section", None, None),
            P("section", None, None),
            P("section", None, None),
            P("section", None),
            P("section", None),
            P("section", None),
        ),
        check_vma=False,
    )
```

profile of v0, /device:TPU:0, one launch (start us, length us, event | category | flops | bytes accessed | tf_op | source)
XLA Modules:
  0.0 1920.7 jit_solution(7976799707412062533)
XLA Ops:
  10.1 44.3 %all-gather.11.cloned.1.call-done = bf16[1,1024,1024]{2,1,0:T(8,128)(2,1)} async-done(((bf16[1,64,1024]{2,1,0:T(8,128)(2,1)}), bf16[1,1024,1024]{2,1,0:T(8,128)(2,1)}) %all-gather.11.cloned.1.call-update) | async-done | bytes 2097168 | tf_op jit(solution)/shard_map/all_gather | solution.py:269
  54.5 59.7 %all-gather.15.cloned.1.call-done = bf16[1,1024,2816]{2,1,0:T(8,128)(2,1)} async-done(((bf16[1,64,2816]{2,1,0:T(8,128)(2,1)}), bf16[1,1024,2816]{2,1,0:T(8,128)(2,1)}) %all-gather.15.cloned.1.call-update) | async-done | bytes 5767184 | tf_op jit(solution)/shard_map/all_gather | solution.py:271
  114.1 75.1 %all-gather.9.cloned.1.call-done = bf16[1,1024,4096]{2,1,0:T(8,128)(2,1)} async-done(((bf16[1,64,4096]{2,1,0:T(8,128)(2,1)}), bf16[1,1024,4096]{2,1,0:T(8,128)(2,1)}) %all-gather.9.cloned.1.call-update) | async-done | bytes 8388624 | tf_op jit(solution)/shard_map/all_gather | solution.py:268
  189.3 94.7 %all-gather.13.cloned.1.call-done = bf16[1,1024,5632]{2,1,0:T(8,128)(2,1)} async-done(((bf16[1,64,5632]{2,1,0:T(8,128)(2,1)}), bf16[1,1024,5632]{2,1,0:T(8,128)(2,1)}) %all-gather.13.cloned.1.call-update) | async-done | bytes 11534352 | tf_op jit(solution)/shard_map/all_gather | solution.py:270
  284.1 139.2 %conditional.4 = (f32[128,1024]{1,0:T(8,128)S(1)}, bf16[128,1024]{1,0:T(8,128)(2,1)S(1)}, f32[128,4096]{1,0:T(8,128)}, f32[128,16]{0,1:T(8,128)S(1)}, bf16[128,1...) conditional(s32[]{:T(128)} %convert_element_type.98, () %tuple.153, ...), branch_computations={%region_0.0_spmd, %region_1.12_spmd} | conditional | flops 4077421824 | bytes 130098896 | solution.py:238
  287.7 4.7 fusion.545
  302.2 100.7 %while.198 = (s32[]{:T(128)}, f32[8,128,128]{2,1,0:T(8,128)S(1)}, f32[2,8,64,128]{3,2,1,0:T(8,128)}, s32[2,64]{1,0:T(2,128)S(1)}, s32[2]{0:T(128)S(1)}, /*index=...) while((s32[]{:T(128)}, f32[8,128,128]{2,1,0:T(8,128)S(1)}, ...), condition=%wide.region_8.9_spmd.clone, body=%wide.region_6.8_spmd.clone.sunk | while | flops 504959104 | bytes 11221944 | solution.py:113
  308.9 40.0 %custom-call.73 = f32[8,1,64,64]{2,3,1,0:T(8,128)S(1)} custom-call(f32[8,1,64,64]{3,2,1,0:T(8,128)} %fusion.869), custom_call_target="InvertDiagBlocksLowerTriangular" | custom-call | tf_op jit(solution)/shard_map/cond/branch_1_fun/while/body/eval_jaxpr/triangular_solve/custom-call.1 | solution.py:89
  359.0 40.0 %custom-call.73 = f32[8,1,64,64]{2,3,1,0:T(8,128)S(1)} custom-call(f32[8,1,64,64]{3,2,1,0:T(8,128)} %fusion.869), custom_call_target="InvertDiagBlocksLowerTriangular" | custom-call | tf_op jit(solution)/shard_map/cond/branch_1_fun/while/body/eval_jaxpr/triangular_solve/custom-call.1 | solution.py:89
  409.1 7.6 fusion.546
  416.7 3.1 fusion.267
  419.8 3.3 convolution_add_fusion.19
  424.7 11.8 collective-permute-done
  437.3 13.6 conditional.5
  451.9 2.6 add.755
  454.6 3.2 add.757
  457.9 3.2 add.758
  463.4 2.5 add.762
  466.9 11.9 conditional.6
  480.4 456.4 %collective-permute-done.1 = bf16[128,1024]{1,0:T(8,128)(2,1)S(1)} collective-permute-done((bf16[128,1024]{1,0:T(8,128)(2,1)S(1)}, bf16[128,1024]{1,0:T(8,128)(2,1)S(1)}, u32[]{:S(2)}, u32[]{:S(2)}) %collective-permute-start.1) | collective-permute-done | bytes 262176 | tf_op jit(solution)/shard_map/ppermute | solution.py:21
  937.0 318.2 %conditional.7 = (f32[128,1024]{1,0:T(8,128)}, f32[1024,16]{0,1:T(8,128)S(1)}, f32[2,1024]{1,0:T(2,128)S(1)}, f32[4,3072]{1,0:T(4,128)S(1)}, f32[8]{0:T(128)S(1)...) conditional(s32[]{:T(128)} %convert_element_type.98, () %tuple.159, ...), branch_computations={%region_58.63_spmd, %region_59.98_spmd} | conditional | flops 5142594560 | bytes 406108192 | solution.py:238
  937.9 4.9 multiply_multiply_fusion.6
  945.3 4.4 multiply_reduce_fusion.29
  959.8 2.6 fusion.486
  977.2 119.9 %while.203 = (s32[]{:T(128)}, f32[8,128,128]{2,1,0:T(8,128)S(1)}, f32[2,8,64,128]{3,2,1,0:T(8,128)}, f32[2,8,64,64]{3,2,1,0:T(8,128)}, f32[2,8,64,64]{3,2,1,0:T(...) while((s32[]{:T(128)}, f32[8,128,128]{2,1,0:T(8,128)S(1)}, ...), condition=%wide.region_65.69_spmd.clone.clone, body=%wide.region_63.68_spmd.clone.clone.sunk | while | flops 505709184 | bytes 33388704 | solution.py:113
  978.3 2.9 bitcast_dynamic-update-slice_fusion.39
  989.4 40.7 %custom-call.69 = f32[8,1,64,64]{2,3,1,0:T(8,128)} custom-call(f32[8,1,64,64]{3,2,1,0:T(8,128)} %get-tuple-element.5641), custom_call_target="InvertDiagBlocksLowerTriangular" | custom-call | tf_op jit(solution)/shard_map/cond/branch_1_fun/jvp()/while/body/eval_jaxpr/triangular_solve/custom-call.1 | solution.py:89
  1030.1 2.8 bitcast_dynamic-update-slice_fusion.38
  1038.1 2.9 bitcast_dynamic-update-slice_fusion.39
  1049.2 40.7 %custom-call.69 = f32[8,1,64,64]{2,3,1,0:T(8,128)} custom-call(f32[8,1,64,64]{3,2,1,0:T(8,128)} %get-tuple-element.5641), custom_call_target="InvertDiagBlocksLowerTriangular" | custom-call | tf_op jit(solution)/shard_map/cond/branch_1_fun/jvp()/while/body/eval_jaxpr/triangular_solve/custom-call.1 | solution.py:89
  1089.9 2.8 bitcast_dynamic-update-slice_fusion.38
  1109.7 122.1 %while.202 = (s32[]{:T(128)}, f32[8,128,128]{2,1,0:T(8,128)S(1)}, f32[2,8,64,128]{3,1,2,0:T(8,128)}, f32[2,8,64,128]{3,1,2,0:T(8,128)}, f32[2,8,64,128]{3,2,1,0:...) while((s32[]{:T(128)}, f32[8,128,128]{2,1,0:T(8,128)S(1)}, ...), condition=%wide.region_80.84_spmd.clone, body=%wide.region_70.83_spmd.clone.sunk | while | flops 1035481152 | bytes 65818020 | solution.py:113
  1118.2 39.3 %custom-call.68 = f32[8,1,64,64]{2,3,1,0:T(8,128)S(1)} custom-call(f32[8,1,64,64]{3,2,1,0:T(8,128)S(1)} %fusion.765), custom_call_target="InvertDiagBlocksLowerTriangular" | custom-call | tf_op jit(solution)/shard_map/cond/branch_1_fun/transpose(jvp())/while/body/eval_jaxpr/triangular_solve/custom-call.0 | solution.py:89
  1158.7 2.3 convolution_add_fusion.48
  1179.0 39.3 %custom-call.68 = f32[8,1,64,64]{2,3,1,0:T(8,128)S(1)} custom-call(f32[8,1,64,64]{3,2,1,0:T(8,128)S(1)} %fusion.765), custom_call_target="InvertDiagBlocksLowerTriangular" | custom-call | tf_op jit(solution)/shard_map/cond/branch_1_fun/transpose(jvp())/while/body/eval_jaxpr/triangular_solve/custom-call.0 | solution.py:89
  1219.5 2.3 convolution_add_fusion.48
  1236.7 2.7 add_add_fusion.7
  1248.3 4.2 fusion.553
  1258.0 3.6 fusion.514
  1261.6 9.1 pad_maximum_fusion.3
  1271.9 9.4 fusion.516
  1281.3 14.6 fusion.512
  1295.9 23.9 %pad_maximum_fusion.2 = f32[1024,8448]{1,0:T(8,128)} fusion(f32[1024,2816]{1,0:T(8,128)} %fusion.516, f32[1024,5632]{1,0:T(8,128)} %fusion.512), kind=kLoop, calls=%fused_computation.948 | loop fusion | flops 8650752 | bytes 69206016 | tf_op jit(solution)/shard_map/concatenate | solution.py:234
  1325.0 63.7 %all-reduce.56 = (f32[1,2,1024]{2,1,0:T(2,128)}, f32[1,4,3072]{2,1,0:T(4,128)}, f32[1,8]{1,0:T(1,128)}, f32[1,8]{1,0:T(1,128)}, f32[1,128]{1,0:T(1,128)}) all-reduce(f32[1,2,1024]{2,1,0:T(2,128)S(1)} %add_bitcast_fusion.6, f32[1,4,3072]{2,1,0:T(4,128)S(1)} %add_bitcast_fusion.5, ...), channel_id=1, replica_groups=mesh['section'=2,'dp'=16] {'dp'}, use_global_device_ids=true, to_apply=%region_97.102 | all-reduce | flops 14480 | bytes 115840 | tf_op jit(solution)/shard_map/psum | solution.py:306
  1388.8 90.9 %reduce-scatter.3.cloned.1.call-done = f32[64,5120]{1,0:T(8,128)} async-done(((f32[1024,5120]{1,0:T(8,128)}), f32[64,5120]{1,0:T(8,128)}) %reduce-scatter.3.cloned.1.call-update) | async-done | bytes 1310736 | tf_op jit(solution)/shard_map/reduce_scatter | solution.py:304
  1483.6 339.2 %reduce-scatter.5.cloned.1.call-done = f32[64,8448]{1,0:T(8,128)} async-done(((f32[1024,8448]{1,0:T(8,128)}), f32[64,8448]{1,0:T(8,128)}) %reduce-scatter.5.cloned.1.call-update) | async-done | bytes 2162704 | tf_op jit(solution)/shard_map/reduce_scatter | solution.py:303
  1822.8 2.6 slice_bitcast_fusion.14
  1827.4 84.8 %all-reduce.59.cloned.1.call-done = f32[1,1024,16]{1,2,0:T(8,128)} async-done(((f32[1,1024,16]{1,2,0:T(8,128)}), f32[1,1024,16]{1,2,0:T(8,128)}) %all-reduce.59.cloned.1.call-update) | async-done | bytes 65552 | tf_op jit(solution)/shard_map/psum | solution.py:306
  (951 shorter events, 197.0 us)
Async XLA Ops:
  7.2 276.9 %copy-start.78 = (f32[128,1024]{1,0:T(8,128)S(1)}, f32[128,1024]{1,0:T(8,128)}, u32[]{:S(2)}) copy-start(f32[128,1024]{1,0:T(8,128)} %param.40) | copy-start | bytes 1572868
  7.2 276.8 %copy-start.220 = (f32[1,2,1024]{2,1,0:T(2,128)S(1)}, f32[1,2,1024]{2,1,0:T(2,128)}, u32[]{:S(2)}) copy-start(f32[1,2,1024]{2,1,0:T(2,128)} %param.48) | copy-start | bytes 24580
  7.2 276.8 %copy-start.202 = (f32[1,4,3072]{2,1,0:T(4,128)S(1)}, f32[1,4,3072]{2,1,0:T(4,128)}, u32[]{:S(2)}) copy-start(f32[1,4,3072]{2,1,0:T(4,128)} %param.49) | copy-start | bytes 147460
  7.2 276.8 %copy-start.346 = (s32[128]{0:T(128)S(1)}, s32[128]{0:T(128)}, u32[]{:S(2)}) copy-start(s32[128]{0:T(128)} %param.42) | copy-start | bytes 1540
  7.2 276.8 %copy-start.203 = (bf16[1,1024,16]{1,2,0:T(8,128)(2,1)S(1)}, bf16[1,1024,16]{1,2,0:T(8,128)(2,1)}, u32[]{:S(2)}) copy-start(bf16[1,1024,16]{1,2,0:T(8,128)(2,1)} %param.47) | copy-start | bytes 98308
  7.2 276.8 %copy-start.349 = (f32[1,8]{1,0:T(1,128)S(1)}, f32[1,8]{1,0:T(1,128)}, u32[]{:S(2)}) copy-start(f32[1,8]{1,0:T(1,128)} %param.50) | copy-start | bytes 100
  7.2 276.8 %copy-start.290 = (f32[1,8]{1,0:T(1,128)S(1)}, f32[1,8]{1,0:T(1,128)}, u32[]{:S(2)}) copy-start(f32[1,8]{1,0:T(1,128)} %param.51) | copy-start | bytes 100
  7.3 276.8 %copy-start.273 = (f32[1,128]{1,0:T(1,128)S(1)}, f32[1,128]{1,0:T(1,128)}, u32[]{:S(2)}) copy-start(f32[1,128]{1,0:T(1,128)} %param.52) | copy-start | bytes 1540
  7.3 47.2 %all-gather.11.cloned.1.call-start = ((), (), s32[]{:S(2)}) async-start(), calls=%async_computation.6 | async-start | bytes 2228224 | tf_op jit(solution)/shard_map/all_gather | solution.py:269
  8.0 106.1 %all-gather.15.cloned.1.call-start = ((), (), s32[]{:S(2)}) async-start(), calls=%async_computation.8 | async-start | bytes 6127616 | tf_op jit(solution)/shard_map/all_gather | solution.py:271
  8.8 180.5 %all-gather.9.cloned.1.call-start = ((), (), s32[]{:S(2)}) async-start(), calls=%async_computation.5 | async-start | bytes 8912896 | tf_op jit(solution)/shard_map/all_gather | solution.py:268
  9.5 274.5 %all-gather.13.cloned.1.call-start = ((), (), s32[]{:S(2)}) async-start(), calls=%async_computation.7 | async-start | bytes 12255232 | tf_op jit(solution)/shard_map/all_gather | solution.py:270
  10.1 1469.6 %reduce-scatter.3.cloned.1.call-start = ((), (), s32[]{:S(2)}) async-start(), calls=%async_computation.2 | async-start | bytes 22282240 | tf_op jit(solution)/shard_map/reduce_scatter | solution.py:304
  406.4 13.4 slice-start.7
  409.1 10.7 slice-start.8
  423.3 13.2 copy-start.181
  423.3 13.2 copy-start.158
  423.3 13.2 copy-start.247
  423.3 13.2 collective-permute-start
  451.9 10.7 copy-start.152
  451.9 14.9 slice-start
  451.9 14.9 copy-start.176
  454.6 12.3 copy-start.208
  454.6 12.2 slice-start.1
  454.6 12.2 copy-start.37
  478.8 458.2 %copy-start.120 = (f32[128,1024]{1,0:T(8,128)}, f32[128,1024]{1,0:T(8,128)S(1)}, u32[]{:S(2)}) copy-start(f32[128,1024]{1,0:T(8,128)S(1)} %get-tuple-element.2867) | copy-start | bytes 1572868
  478.8 458.2 %copy-start.191 = (bf16[128,1024]{1,0:T(8,128)(2,1)}, bf16[128,1024]{1,0:T(8,128)(2,1)S(1)}, u32[]{:S(2)}) copy-start(bf16[128,1024]{1,0:T(8,128)(2,1)S(1)} %get-tuple-element.2877) | copy-start | bytes 786436
  478.8 458.2 %copy-start.193 = (bf16[128,1024]{1,0:T(8,128)(2,1)}, bf16[128,1024]{1,0:T(8,128)(2,1)S(1)}, u32[]{:S(2)}) copy-start(bf16[128,1024]{1,0:T(8,128)(2,1)S(1)} %get-tuple-element.2869) | copy-start | bytes 786436
  478.8 458.2 %copy-start.195 = (bf16[128,1024]{1,0:T(8,128)(2,1)}, bf16[128,1024]{1,0:T(8,128)(2,1)S(1)}, u32[]{:S(2)}) copy-start(bf16[128,1024]{1,0:T(8,128)(2,1)S(1)} %get-tuple-element.2873) | copy-start | bytes 786436
  478.8 458.2 %copy-start.206 = (f32[1024,16]{0,1:T(8,128)}, f32[1024,16]{0,1:T(8,128)S(1)}, u32[]{:S(2)}) copy-start(f32[1024,16]{0,1:T(8,128)S(1)} %get-tuple-element.2885) | copy-start | bytes 196612
  478.8 458.2 %copy-start.218 = (f32[4,3072]{1,0:T(4,128)}, f32[4,3072]{1,0:T(4,128)S(1)}, u32[]{:S(2)}) copy-start(f32[4,3072]{1,0:T(4,128)S(1)} %get-tuple-element.2889) | copy-start | bytes 147460
  478.8 458.2 %copy-start.279 = (f32[2,1024]{1,0:T(2,128)}, f32[2,1024]{1,0:T(2,128)S(1)}, u32[]{:S(2)}) copy-start(f32[2,1024]{1,0:T(2,128)S(1)} %get-tuple-element.2887) | copy-start | bytes 24580
  478.8 458.2 %copy-start.342 = (f32[8]{0:T(128)}, f32[8]{0:T(128)S(1)}, u32[]{:S(2)}) copy-start(f32[8]{0:T(128)S(1)} %get-tuple-element.2891) | copy-start | bytes 100
  478.9 458.2 %copy-start.344 = (f32[8]{0:T(128)}, f32[8]{0:T(128)S(1)}, u32[]{:S(2)}) copy-start(f32[8]{0:T(128)S(1)} %get-tuple-element.2893) | copy-start | bytes 100
  478.9 458.2 %copy-start.363 = (f32[128]{0:T(128)}, f32[128]{0:T(128)S(1)}, u32[]{:S(2)}) copy-start(f32[128]{0:T(128)S(1)} %get-tuple-element.2895) | copy-start | bytes 1540
  478.9 458.0 %copy-start.32 = (f32[128,1024]{1,0:T(8,128)S(1)}, f32[128,1024]{1,0:T(8,128)}, u32[]{:S(2)}) copy-start(f32[128,1024]{1,0:T(8,128)} %copy-done.31) | copy-start | bytes 1572868
  478.9 458.0 %copy-start.209 = (f32[128,16]{0,1:T(8,128)S(1)}, f32[128,16]{0,1:T(8,128)}, u32[]{:S(2)}) copy-start(f32[128,16]{0,1:T(8,128)} %copy-done.208) | copy-start | bytes 24580
  478.9 458.0 %copy-start.222 = (f32[1,2,1024]{2,1,0:T(2,128)S(1)}, f32[1,2,1024]{2,1,0:T(2,128)}, u32[]{:S(2)}) copy-start(f32[1,2,1024]{2,1,0:T(2,128)} %param.48) | copy-start | bytes 24580
  478.9 458.0 %copy-start.292 = (f32[1,8]{1,0:T(1,128)S(1)}, f32[1,8]{1,0:T(1,128)}, u32[]{:S(2)}) copy-start(f32[1,8]{1,0:T(1,128)} %param.51) | copy-start | bytes 100
  478.9 458.0 %copy-start.348 = (s32[128]{0:T(128)S(1)}, s32[128]{0:T(128)}, u32[]{:S(2)}) copy-start(s32[128]{0:T(128)} %param.42) | copy-start | bytes 1540
  478.9 458.0 %copy-start.351 = (f32[1,8]{1,0:T(1,128)S(1)}, f32[1,8]{1,0:T(1,128)}, u32[]{:S(2)}) copy-start(f32[1,8]{1,0:T(1,128)} %param.50) | copy-start | bytes 100
  479.0 457.8 %collective-permute-start.1 = (bf16[128,1024]{1,0:T(8,128)(2,1)S(1)}, bf16[128,1024]{1,0:T(8,128)(2,1)S(1)}, u32[]{:S(2)}, u32[]{:S(2)}) collective-permute-start(bf16[128,1024]{1,0:T(8,128)(2,1)S(1)} %convert_element_type.100), channel_id=1, source_target_pairs={{16,0},{17,1},{18,2},{19,3},{20,4},{21,5},{22,6},{23,7},{24,8},{25... | collective-permute-start | bytes 786440 | tf_op jit(solution)/shard_map/ppermute | solution.py:21
  937.1 19.7 %copy-start.355 = (f32[8]{0:T(128)}, f32[8]{0:T(128)S(1)}, u32[]{:S(2)}) copy-start(f32[8]{0:T(128)S(1)} %get-tuple-element.2739) | copy-start | bytes 100 | tf_op jit(solution)/shard_map/cond
  937.1 19.7 %copy-start.212 = (f32[128,16]{0,1:T(8,128)}, f32[128,16]{0,1:T(8,128)S(1)}, u32[]{:S(2)}) copy-start(f32[128,16]{0,1:T(8,128)S(1)} %get-tuple-element.2740) | copy-start | bytes 24580 | tf_op jit(solution)/shard_map/cond
  937.1 19.7 %copy-start.296 = (f32[1,8]{1,0:T(1,128)}, f32[1,8]{1,0:T(1,128)S(1)}, u32[]{:S(2)}) copy-start(f32[1,8]{1,0:T(1,128)S(1)} %get-tuple-element.2741) | copy-start | bytes 100 | tf_op jit(solution)/shard_map/cond
  1109.7 123.7 %copy-start.268 = (f32[128,8]{0,1:T(8,128)S(1)}, f32[128,8]{0,1:T(8,128)}, u32[]{:S(2)}) copy-start(f32[128,8]{0,1:T(8,128)} %copy-done.267) | copy-start | bytes 12292 | tf_op jit(solution)/shard_map/cond
  1270.7 552.2 %reduce-scatter.5.cloned.1.call-start = ((), (), s32[]{:S(2)}) async-start(), calls=%async_computation.3 | async-start | bytes 36765696 | tf_op jit(solution)/shard_map/reduce_scatter | solution.py:303
  1319.8 592.3 %all-reduce.59.cloned.1.call-start = ((), (), s32[]{:S(2)}) async-start(), calls=%async_computation.4 | async-start | bytes 131072 | tf_op jit(solution)/shard_map/psum | solution.py:306
  (234 other events, 635.7 us)
Sparse Core Ops, SparseCore 0:
  10.2 44.1 all-gather.10
  56.7 57.3 all-gather.14
  116.3 72.9 all-gather.8
  191.4 92.5 all-gather.12
  1270.8 208.8 reduce-scatter.2
  1483.8 338.9 reduce-scatter.4
  1826.9 85.2 all-reduce.58
where the time goes:
time: 1930 us; the launch traced here: 1920 us
  waiting for transfers between devices  1260 us (65%)
  other arithmetic  345 us (18%)
  matrix products  130 us (7%)
  local copies, waits for them, and re-layouts  83.6 us (4%)
  blocking collectives  63.7 us (3%)
  loops' own time  19.5 us (1%)
    ppermute x2, waiting for transfers between devices, passed_along(): lax.ppermute(value, axis, [(source, source + steps) for source in range(i...  468 us
    reduce_scatter x1, waiting for transfers between devices, local(): lax.psum_scatter(ffn_terms(factors), 'dp', scatter_dimension=0, tiled=True)  339 us
    another operation x26, other arithmetic, step_block(): lax.linalg.triangular_solve(left_side, right_side, left_side=True, lower=...  241 us
    all_gather x1, waiting for transfers between devices, local(): lax.all_gather(w_up[0], 'dp', axis=0, tiled=True)  94.7 us
    reduce_scatter x1, waiting for transfers between devices, local(): lax.psum_scatter(mixer_terms(factors), 'dp', scatter_dimension=0, tiled=T...  90.9 us
    psum x1, waiting for transfers between devices, local(): small_sums = lax.psum(small_local, 'dp')  84.8 us
    all_gather x1, waiting for transfers between devices, local(): lax.all_gather(w_in[0], 'dp', axis=0, tiled=True)  75.1 us
    psum x1, blocking collectives, local(): small_sums = lax.psum(small_local, 'dp')  63.7 us
  transfers between devices with their start and end apart: 9, of which 9 were waited for; matrix products, arithmetic and copies ran while one was open for 3% of the time, Pallas kernels for 0%

commit v1 on v0

v1 whole, which is shorter than its diff:
```python
import jax
import jax.numpy as jnp
from jax import lax
from jax.experimental import pallas as pl
from jax.sharding import PartitionSpec as P

D = 1024
FF = 2816
HEADS = 8
HEAD_DIM = 128
CONV = 4
BLOCK = 128
GROUP_HEADS = 4


epsilon = 1e-06
highest = lax.Precision.HIGHEST


def passed_along(value, axis, steps):
    count = lax.axis_size(axis)
    initial, last = (max(0, -steps), min(count, count - steps))
    return lax.ppermute(value, axis, [(source, source + steps) for source in range(initial, last)])


def dot_rows(left, right):
    return lax.dot_general(
        left, right, (((1,), (1,)), ((), ())), preferred_element_type=jnp.float32
    )


def dot_cols(left, right):
    return lax.dot_general(
        left, right, (((0,), (0,)), ((), ())), preferred_element_type=jnp.float32
    )


def rms_scale(values, gain):
    return values * lax.rsqrt(jnp.mean(values * values, axis=-1, keepdims=True) + epsilon) * gain


def segment_ids(marks_block):
    position = jnp.arange(marks_block.shape[0])
    starts = jnp.logical_or(marks_block > 0, position == 0).astype(jnp.int32)
    return jnp.cumsum(starts)


def short_conv(columns, kernel, segment):
    row_count, width = columns.shape
    total = columns * kernel[CONV - 1]
    for offset in range(1, CONV):
        shifted = jnp.concatenate(
            [jnp.zeros((offset, width), columns.dtype), columns[: row_count - offset]], axis=0
        )
        same = jnp.concatenate(
            [jnp.zeros((offset,), jnp.bool_), segment[offset:] == segment[: row_count - offset]]
        )
        total = total + jnp.where(same[:, None], shifted, 0.0) * kernel[CONV - 1 - offset]
    return jax.nn.silu(total)


def triangle(seg_col, seg_row):
    row = lax.broadcasted_iota(jnp.int32, (BLOCK, BLOCK), 0)
    col = lax.broadcasted_iota(jnp.int32, (BLOCK, BLOCK), 1)
    within = jnp.logical_and(seg_col == seg_row, row >= col)
    return row, col, within


def mm(left, right, dims):
    return lax.dot_general(
        left, right, (dims, ((), ())), precision=highest, preferred_element_type=jnp.float32
    )


NN = ((1,), (0,))
NT = ((1,), (1,))
TN = ((0,), (0,))


def delta_fwd_kernel(
    q_ref, k_ref, v_ref, beta_ref, ccol_ref, crow_ref, scol_ref, srow_ref, o_ref, t_ref, p_ref
):
    row, col, within = triangle(scol_ref[...], srow_ref[0])
    apart = jnp.bitwise_xor(row, col)
    eye = (row == col).astype(jnp.float32)
    heads = range(GROUP_HEADS)
    at = [pl.ds(h * HEAD_DIM, HEAD_DIM) for h in heads]
    weights = [
        jnp.where(within, jnp.exp(jnp.minimum(ccol_ref[h] - crow_ref[h], 0.0)), 0.0) for h in heads
    ]
    keys = [k_ref[:, at[h]] for h in heads]
    below = [
        jnp.where(row > col, weights[h], 0.0) * mm(keys[h], keys[h], NT) * beta_ref[h]
        for h in heads
    ]
    inverse = [eye - jnp.where(apart == 1, below[h], 0.0) for h in heads]
    size = 2
    while size < BLOCK:
        level = jnp.logical_and(apart >= size, apart < 2 * size)
        inner = [mm(jnp.where(level, below[h], 0.0), inverse[h], NN) for h in heads]
        inverse = [inverse[h] - mm(inverse[h], inner[h], NN) for h in heads]
        size *= 2
    pseudo = [mm(inverse[h], beta_ref[h] * v_ref[:, at[h]], NN) for h in heads]
    for h in heads:
        score = mm(q_ref[:, at[h]], keys[h], NT) * weights[h]
        o_ref[:, at[h]] = mm(score, pseudo[h], NN)
        t_ref[:, at[h]] = inverse[h]
        p_ref[:, at[h]] = pseudo[h]


def delta_bwd_kernel(
    q_ref,
    k_ref,
    v_ref,
    beta_ref,
    ccol_ref,
    crow_ref,
    scol_ref,
    srow_ref,
    t_ref,
    p_ref,
    do_ref,
    dq_ref,
    dk_ref,
    dv_ref,
    dbeta_ref,
    dccol_ref,
    dcrow_ref,
):
    row, col, within = triangle(scol_ref[...], srow_ref[0])
    strict = row > col
    for h in range(GROUP_HEADS):
        at = pl.ds(h * HEAD_DIM, HEAD_DIM)
        weights = jnp.where(within, jnp.exp(jnp.minimum(ccol_ref[h] - crow_ref[h], 0.0)), 0.0)
        query, key, value, beta = q_ref[:, at], k_ref[:, at], v_ref[:, at], beta_ref[h]
        pseudo, d_out = p_ref[:, at], do_ref[:, at]
        key_key = mm(key, key, NT)
        query_key = mm(query, key, NT)
        d_score = mm(d_out, pseudo, NT)
        d_pseudo = mm(query_key * weights, d_out, TN)
        d_right = mm(t_ref[:, at], d_pseudo, TN)
        d_left = jnp.where(strict, -mm(d_right, pseudo, NT), 0.0)
        dv_ref[:, at] = beta * d_right
        left_key = d_left * weights
        dbeta_ref[h] = jnp.sum(d_right * value, axis=1, keepdims=True) + jnp.sum(
            left_key * key_key, axis=1, keepdims=True
        )
        d_query_key = d_score * weights
        d_key_key = left_key * beta
        dq_ref[:, at] = mm(d_query_key, key, NN)
        dk_ref[:, at] = (
            mm(d_query_key, query, TN) + mm(d_key_key, key, NN) + mm(d_key_key, key, TN)
        )
        d_spread = d_query_key * query_key + d_key_key * key_key
        dccol_ref[h] = jnp.sum(d_spread, axis=1, keepdims=True)
        dcrow_ref[h] = jnp.sum(d_spread, axis=0, keepdims=True)


def delta_call(kernel, ins, kinds, outs, flops):
    rows = ins[0].shape[0]
    wide = pl.BlockSpec((BLOCK, GROUP_HEADS * HEAD_DIM), lambda b, g: (b, g))
    column = pl.BlockSpec((GROUP_HEADS, BLOCK, 1), lambda b, g: (g, b, 0))
    flat = pl.BlockSpec((GROUP_HEADS, 1, BLOCK), lambda b, g: (g, 0, b))
    seg_column = pl.BlockSpec((BLOCK, 1), lambda b, g: (b, 0))
    seg_flat = pl.BlockSpec((1, 1, BLOCK), lambda b, g: (0, 0, b))
    specs = {"w": wide, "c": column, "r": flat, "s": seg_column, "t": seg_flat}
    shapes = {"w": (rows, HEADS * HEAD_DIM), "c": (HEADS, rows, 1), "r": (HEADS, 1, rows)}
    return pl.pallas_call(
        kernel,
        grid=(rows // BLOCK, HEADS // GROUP_HEADS),
        in_specs=[specs[kind] for kind in kinds],
        out_specs=[specs[kind] for kind in outs],
        out_shape=[jax.ShapeDtypeStruct(shapes[kind], jnp.float32) for kind in outs],
        cost_estimate=pl.CostEstimate(
            flops=flops * rows * BLOCK * D, bytes_accessed=40 * rows * D, transcendentals=rows * D
        ),
    )(*ins)


@jax.custom_vjp
def delta_core(queries, keys, values, beta, cumul, segment):
    return delta_core_fwd(queries, keys, values, beta, cumul, segment)[0]


def delta_core_fwd(queries, keys, values, beta, cumul, segment):
    ins = (
        queries,
        keys,
        values,
        beta.T[:, :, None],
        cumul.T[:, :, None],
        cumul.T[:, None, :],
        segment[:, None],
        segment[None, None, :],
    )
    out, inverse, pseudo = delta_call(delta_fwd_kernel, ins, "wwwccrst", "www", 200)
    return out, (ins, inverse, pseudo)


def delta_core_bwd(saved, d_out):
    ins, inverse, pseudo = saved
    d_q, d_k, d_v, d_beta, d_col, d_row = delta_call(
        delta_bwd_kernel, ins + (inverse, pseudo, d_out), "wwwccrstwww", "wwwccr", 120
    )
    d_cumul = (d_col[:, :, 0] - d_row[:, 0, :]).T
    return d_q, d_k, d_v, d_beta[:, :, 0].T, d_cumul, None


delta_core.defvjp(delta_core_fwd, delta_core_bwd)


def delta_rule(queries, key_rows, value_rows, beta_rows, log_decay, segment):
    rows = queries.shape[0]
    cumul = jnp.cumsum(log_decay.reshape(rows // BLOCK, BLOCK, HEADS), axis=1).reshape(rows, HEADS)

    def wide(array):
        return array.reshape(rows, HEADS * HEAD_DIM)

    out = delta_core(
        wide(queries), wide(key_rows), wide(value_rows), beta_rows, cumul, segment
    )
    return out.reshape(rows, HEADS, HEAD_DIM)


def mixer_core(proj, gate_pre, kernel, decay_log, decay_bias, out_gain, segment):
    row_count = proj.shape[0]
    mixed_in = short_conv(proj[:, : 3 * D], kernel, segment)
    heads_shape = (row_count, HEADS, HEAD_DIM)
    query_raw = mixed_in[:, :D].reshape(heads_shape)
    key_raw = mixed_in[:, D : 2 * D].reshape(heads_shape)
    value_rows = mixed_in[:, 2 * D :].reshape(heads_shape)
    queries = (
        query_raw
        * lax.rsqrt(jnp.sum(query_raw * query_raw, axis=-1, keepdims=True) + epsilon)
        * HEAD_DIM ** (-0.5)
    )
    key_rows = key_raw * lax.rsqrt(jnp.sum(key_raw * key_raw, axis=-1, keepdims=True) + epsilon)
    beta_rows = jax.nn.sigmoid(gate_pre[:, HEADS:])
    log_decay = -jnp.exp(decay_log) * jax.nn.softplus(gate_pre[:, :HEADS] + decay_bias)
    delta_out = delta_rule(queries, key_rows, value_rows, beta_rows, log_decay, segment)
    scaled = (
        delta_out
        * lax.rsqrt(jnp.mean(delta_out * delta_out, axis=-1, keepdims=True) + epsilon)
        * out_gain
    )
    gate_part = proj[:, 3 * D :].reshape(heads_shape)
    return (scaled * jax.nn.silu(gate_part)).reshape(row_count, D)


def swiglu(upgate):
    return jax.nn.silu(upgate[:, :FF]) * upgate[:, FF:]


def layer_forward(weights, small_params, block, segment):
    w_in, w_out, w_up, w_down = weights
    gate_weights, norm_gains, kernel, decay_log, decay_bias, out_gain = small_params
    normed_a = rms_scale(block, norm_gains[0]).astype(jnp.bfloat16)
    proj = jnp.dot(normed_a, w_in, preferred_element_type=jnp.float32)
    gate_pre = jnp.dot(normed_a, gate_weights, preferred_element_type=jnp.float32)

    def core_of(proj_in, gate_in, kernel_in, log_in, bias_in, gain_in):
        return mixer_core(proj_in, gate_in, kernel_in, log_in, bias_in, gain_in, segment)

    mixer, core_back = jax.vjp(
        core_of, proj, gate_pre, kernel, decay_log, decay_bias, out_gain
    )
    mixer = mixer.astype(jnp.bfloat16)
    middle = block + jnp.dot(mixer, w_out, preferred_element_type=jnp.float32)
    normed_f = rms_scale(middle, norm_gains[1]).astype(jnp.bfloat16)
    upgate = jnp.dot(normed_f, w_up, preferred_element_type=jnp.float32)
    hidden = swiglu(upgate).astype(jnp.bfloat16)
    result = middle + dot_rows(hidden, w_down)
    return (result, (normed_a, core_back, mixer, middle, normed_f, upgate, hidden))


def summed_rows(left, right):
    part = dot_cols(left, right).astype(jnp.bfloat16)
    return lax.psum_scatter(part, "dp", scatter_dimension=0, tiled=True).astype(jnp.float32)


def layer_backward(weights, small_params, block, saved, grad_out, sums):
    w_in, w_out, w_up, w_down = weights
    gate_weights, norm_gains = small_params[:2]
    normed_a, core_back, mixer, middle, normed_f, upgate, hidden = saved
    g_bf = grad_out.astype(jnp.bfloat16)
    d_hidden = jnp.dot(g_bf, w_down, preferred_element_type=jnp.float32)
    _, swiglu_back = jax.vjp(swiglu, upgate)
    d_upgate = swiglu_back(d_hidden)[0].astype(jnp.bfloat16)
    d_normed_f = dot_rows(d_upgate, w_up)
    _, norm_back_f = jax.vjp(rms_scale, middle, norm_gains[1])
    d_middle, gain_f = norm_back_f(d_normed_f)
    d_middle = d_middle + grad_out
    dm_bf = d_middle.astype(jnp.bfloat16)
    d_mixer = dot_rows(dm_bf, w_out)
    d_proj, d_gate_pre, d_kernel, d_log, d_bias, d_gain = core_back(d_mixer)
    d_proj = d_proj.astype(jnp.bfloat16)
    d_gate_pre = d_gate_pre.astype(jnp.bfloat16)
    d_normed_a = dot_rows(d_proj, w_in) + dot_rows(d_gate_pre, gate_weights)
    _, norm_back_a = jax.vjp(rms_scale, block, norm_gains[0])
    d_block, gain_a = norm_back_a(d_normed_a)
    d_block = d_block + d_middle
    if not sums:
        return d_block
    big = (
        summed_rows(normed_a, d_proj),
        summed_rows(mixer, dm_bf),
        summed_rows(normed_f, d_upgate),
        summed_rows(g_bf, hidden),
    )
    small = (
        dot_cols(normed_a, d_gate_pre),
        jnp.stack([gain_a, gain_f]),
        d_kernel,
        d_log,
        d_bias,
        d_gain,
    )
    return (d_block, big, small)


def summed_small(parts):
    flat = jnp.concatenate([part.reshape(-1) for part in parts])
    flat = lax.psum(flat, "dp")
    outs, start = [], 0
    for part in parts:
        outs.append(flat[start : start + part.size].reshape(part.shape))
        start += part.size
    return outs


def local(
    block_input,
    cotangent,
    marks,
    w_in,
    w_out,
    w_up,
    w_down,
    gate_weights,
    norm_gains,
    conv_weights,
    decay_log,
    decay_bias,
    out_gain,
):
    first_section = lax.axis_index("section") == 0
    small_params = (
        gate_weights[0],
        norm_gains[0],
        conv_weights[0],
        decay_log[0],
        decay_bias[0],
        out_gain[0],
    )
    weights = tuple(
        lax.all_gather(weight[0], "dp", axis=0, tiled=True) for weight in (w_in, w_out, w_up, w_down)
    )
    segment = segment_ids(marks)
    early_out, _ = layer_forward(weights, small_params, block_input, segment)
    arrived = passed_along(early_out.astype(jnp.bfloat16), "section", 1).astype(jnp.float32)
    source = jnp.where(first_section, block_input, arrived)
    layer_out, saved = layer_forward(weights, small_params, source, segment)
    late_grad = layer_backward(weights, small_params, source, saved, cotangent, False)
    returned = passed_along(late_grad.astype(jnp.bfloat16), "section", -1).astype(jnp.float32)
    grad_out = jnp.where(first_section, returned, cotangent)
    input_grad, big, small = layer_backward(weights, small_params, source, saved, grad_out, True)
    return tuple(part[None] for part in (layer_out, input_grad, *big, *summed_small(small)))


def solution(mesh):
    return jax.shard_map(
        local,
        mesh=mesh,
        in_specs=(
            P("dp", None),
            P("dp", None),
            P("dp"),
            P("section", "dp", None),
            P("section", "dp", None),
            P("section", "dp", None),
            P("section", "dp", None),
            P("section", None, None),
            P("section", None, None),
            P("section", None, None),
            P("section", None),
            P("section", None),
            P("section", None),
        ),
        out_specs=(
            P("section", "dp", None),
            P("section", "dp", None),
            P("section", "dp", None),
            P("section", "dp", None),
            P("section", "dp", None),
            P("section", "dp", None),
            P("section", None, None),
            P("section", None, None),
            P("section", None, None),
            P("section", None),
            P("section", None),
            P("section", None),
        ),
        check_vma=False,
    )
```

time: 1930 us -> 975 us (0.51)
  waiting for transfers between devices: 1260 us -> 675 us
  other arithmetic: 345 us -> 78 us
  blocking collectives: 63.7 us -> 0 us
  Pallas kernels: 0 us -> 55.3 us
  local copies, waits for them, and re-layouts: 83.6 us -> 46.2 us
  matrix products: 130 us -> 93 us
  loops' own time: 19.5 us -> 0 us
    ppermute x2, waiting for transfers between devices: 468 us -> 12.4 us  [passed_along(): lax.ppermute(value, axis, [(source, source + steps) for source in range(i...]
    another operation x58 -> x5, other arithmetic: 243 us -> 2.6 us  [the longest x4 2.57 us: delta_rule(): jnp.cumsum(log_decay.reshape(rows // BLOCK, BLOCK, HEADS), axis=1)]
    psum x1 -> x0, blocking collectives: 63.7 us -> none  [local(): small_sums = lax.psum(small_local, 'dp')]
    dot_general x50 -> x0, matrix products: 58.2 us -> none  [the longest x8 15.2 us: step_block(): state_query = jnp.einsum('hid,hed->hie', query_b, state, precision=highest)]
    pallas_call x0 -> x4, Pallas kernels: none -> 55.3 us  [the longest x2 27.9 us: delta_call(): pl.pallas_call(kernel, grid=(rows // BLOCK, HEADS // GROUP_HEADS), in_spe...]
    reduce_scatter x2 -> x4, waiting for transfers between devices: 430 us -> 377 us  [summed_rows(): lax.psum_scatter(part, 'dp', scatter_dimension=0, tiled=True)]
    all_gather x4, waiting for transfers between devices: 274 us -> 230 us  [local(): lax.all_gather(weight[0], 'dp', axis=0, tiled=True)]
    concatenate x4 -> x0, other arithmetic: 35.5 us -> none  [the longest x1 23.9 us: ffn_terms(): jnp.concatenate([dot_cols(normed_f, d_upgate), dot_cols(g_bf, hidden)], a...]
  transfers between devices with their start and end apart: 9 -> 11, of which waited for: 9 -> 11; matrix products, arithmetic and copies ran while one was open for 3% -> 7% of each run, Pallas kernels for 0% -> 1%
where the time goes in v1:
time: 975 us; the launch traced here: 969 us
  waiting for transfers between devices  675 us (69%)
  matrix products  93 us (10%)
  other arithmetic  78 us (8%)
  Pallas kernels  55.3 us (6%)
  local copies, waits for them, and re-layouts  46.2 us (5%)
  between operations  15.8 us (2%)
    reduce_scatter x4, waiting for transfers between devices, summed_rows(): lax.psum_scatter(part, 'dp', scatter_dimension=0, tiled=True)  377 us
    all_gather x4, waiting for transfers between devices, local(): lax.all_gather(weight[0], 'dp', axis=0, tiled=True)  230 us
    psum x1, waiting for transfers between devices, summed_small(): flat = lax.psum(flat, 'dp')  53.2 us
    dot_general x10, matrix products, dot_rows(): lax.dot_general(left, right, (((1,), (1,)), ((), ())), preferred_element_...  36.5 us
    pallas_call x2, Pallas kernels, delta_call(): pl.pallas_call(kernel, grid=(rows // BLOCK, HEADS // GROUP_HEADS), in_spe...  27.9 us
    pallas_call x2, Pallas kernels, delta_rule(): delta_core(wide(queries), wide(key_rows), wide(value_rows), beta_rows, cu...  27.4 us
    unnamed x180, local copies, waits for them, and re-layouts  23.3 us
    dot_general x5, matrix products, dot_cols(): lax.dot_general(left, right, (((0,), (0,)), ((), ())), preferred_element_...  21 us
  transfers between devices with their start and end apart: 11, of which 11 were waited for; matrix products, arithmetic and copies ran while one was open for 7% of the time, Pallas kernels for 1%

profile of v1, /device:TPU:0, one launch (start us, length us, event | category | flops | bytes accessed | tf_op | source)
XLA Modules:
  0.0 968.9 jit_solution(13509978994026980606)
XLA Ops:
  14.6 72.7 %all-gather.9.cloned.1.call-done = bf16[1,1024,4096]{2,1,0:T(8,128)(2,1)} async-done(((bf16[1,64,4096]{2,1,0:T(8,128)(2,1)}), bf16[1,1024,4096]{2,1,0:T(8,128)(2,1)}) %all-gather.9.cloned.1.call-update) | async-done | bytes 8388624 | tf_op jit(solution)/shard_map/all_gather | solution.py:356
  87.3 4.7 fusion.14
  97.6 2.7 fusion.139
  100.3 13.9 %jvp__.2 = (f32[128,1024]{1,0:T(8,128)}, f32[128,1024]{1,0:T(8,128)}, f32[128,1024]{1,0:T(8,128)}) custom-call(f32[128,1024]{1,0:T(8,128)} %get-tuple-element.146.q_ref, f32[128,1024]{1,0:T(8,128)} %get-tuple-element.147.k_ref, f32[128,1024]{1,0:T(8,128)} %get-tuple-element.145.v_ref, f32[8,128,1]{2,1,0:T(8,128)} %copy.139.beta_ref, ...), custom_call_target="tpu_custom_call" | custom-call | flops 3355443200 | bytes 5242880 | tf_op jit(solution)/shard_map/jvp()/pallas_call | solution.py:168
  115.7 14.0 %all-gather.11.cloned.1.call-done = bf16[1,1024,1024]{2,1,0:T(8,128)(2,1)} async-done(((bf16[1,64,1024]{2,1,0:T(8,128)(2,1)}), bf16[1,1024,1024]{2,1,0:T(8,128)(2,1)}) %all-gather.11.cloned.1.call-update) | async-done | bytes 2097168 | tf_op jit(solution)/shard_map/all_gather | solution.py:356
  130.0 2.4 multiply_reduce_fusion.16
  132.4 92.2 %all-gather.13.cloned.1.call-done = bf16[1,1024,5632]{2,1,0:T(8,128)(2,1)} async-done(((bf16[1,64,5632]{2,1,0:T(8,128)(2,1)}), bf16[1,1024,5632]{2,1,0:T(8,128)(2,1)}) %all-gather.13.cloned.1.call-update) | async-done | bytes 11534352 | tf_op jit(solution)/shard_map/all_gather | solution.py:356
  224.6 7.6 fusion.6
  232.2 51.5 %all-gather.15.cloned.1.call-done = bf16[1,1024,2816]{2,1,0:T(8,128)(2,1)} async-done(((bf16[1,64,2816]{2,1,0:T(8,128)(2,1)}), bf16[1,1024,2816]{2,1,0:T(8,128)(2,1)}) %all-gather.15.cloned.1.call-update) | async-done | bytes 5767184 | tf_op jit(solution)/shard_map/all_gather | solution.py:356
  283.7 5.5 fusion.63
  289.2 3.6 collective-permute-start
  294.4 4.1 collective-permute-done
  299.6 4.7 fusion.12
  310.6 5.0 fusion.42
  320.1 2.7 fusion.138
  322.7 14.0 %jvp__.3 = (f32[128,1024]{1,0:T(8,128)}, f32[128,1024]{1,0:T(8,128)}, f32[128,1024]{1,0:T(8,128)}) custom-call(f32[128,1024]{1,0:T(8,128)} %get-tuple-element.141.q_ref, f32[128,1024]{1,0:T(8,128)} %get-tuple-element.142.k_ref, f32[128,1024]{1,0:T(8,128)} %get-tuple-element.140.v_ref, f32[8,128,1]{2,1,0:T(8,128)} %copy.149.beta_ref, ...), custom_call_target="tpu_custom_call" | custom-call | flops 3355443200 | bytes 5242880 | tf_op jit(solution)/shard_map/jvp()/pallas_call | solution.py:168
  338.6 2.3 multiply_convert_fusion.2
  342.4 6.3 fusion.4
  348.8 2.9 fusion.136
  353.4 6.4 multiply_reduce_fusion.12
  364.5 3.0 multiply_add_fusion.8
  367.5 13.7 %transpose_jvp___.2 = (f32[128,1024]{1,0:T(8,128)}, f32[128,1024]{1,0:T(8,128)}, f32[128,1024]{1,0:T(8,128)}, f32[8,128,1]{2,1,0:T(8,128)}, f32[8,128,1]{2,1,0:T(8,128)}, /*index=5*/f32[8,1,128]{2,1,0:T(1,128)}) custom-call(f32[128,1024]{1,0:T(8,128)} %get-tuple-element.141.q_ref, f32[128,1024]{1,0:T(8,128)} %get-tuple-element.142.k_ref, ...), custom_call_target="tpu_custom_call" | custom-call | flops 2013265920 | bytes 5242880 | tf_op jit(solution)/shard_map/transpose(jvp())/pallas_call | solution.py:219
  389.5 2.9 add_add_fusion.7
  395.3 1.8 add_add_fusion.6
  401.7 2.9 fusion.10
  407.2 8.3 collective-permute-done.1
  415.6 6.0 fusion.135
  421.7 6.4 multiply_reduce_fusion.5
  432.6 3.1 multiply_reduce_fusion.4
  435.8 13.8 %transpose_jvp___.3 = (f32[128,1024]{1,0:T(8,128)}, f32[128,1024]{1,0:T(8,128)}, f32[128,1024]{1,0:T(8,128)}, f32[8,128,1]{2,1,0:T(8,128)}, f32[8,128,1]{2,1,0:T(8,128)}, /*index=5*/f32[8,1,128]{2,1,0:T(1,128)}) custom-call(f32[128,1024]{1,0:T(8,128)} %get-tuple-element.141.q_ref, f32[128,1024]{1,0:T(8,128)} %get-tuple-element.142.k_ref, ...), custom_call_target="tpu_custom_call" | custom-call | flops 2013265920 | bytes 5242880 | tf_op jit(solution)/shard_map/transpose(jvp())/pallas_call | solution.py:219
  453.3 2.9 add_add_fusion.2
  458.8 1.8 add_add_fusion.1
  461.0 3.9 multiply_reduce_fusion.3
  473.1 2.9 multiply_add_fusion
  476.0 6.8 fusion.8
  484.8 2.0 convolution_convert_fusion.3
  488.0 4.2 convolution_convert_fusion.2
  493.7 6.7 convolution_convert_fusion.1
  501.7 7.8 convolution_convert_fusion
  511.7 5.4 fusion.60
  517.1 53.2 %all-reduce.38.cloned.1.call-done = f32[30864]{0:T(1024)} async-done(((f32[30864]{0:T(1024)}), f32[30864]{0:T(1024)}) %all-reduce.38.cloned.1.call-update) | async-done | bytes 123472 | tf_op jit(solution)/shard_map/psum | solution.py:323
  577.4 60.4 %reduce-scatter.7.cloned.1.call-done = bf16[64,1024]{1,0:T(8,128)(2,1)} async-done(((bf16[1024,1024]{1,0:T(8,128)(2,1)}), bf16[64,1024]{1,0:T(8,128)(2,1)}) %reduce-scatter.7.cloned.1.call-update) | async-done | bytes 131088 | tf_op jit(solution)/shard_map/reduce_scatter | solution.py:278
  639.5 82.7 %reduce-scatter.11.cloned.1.call-done = bf16[64,2816]{1,0:T(8,128)(2,1)} async-done(((bf16[1024,2816]{1,0:T(8,128)(2,1)}), bf16[64,2816]{1,0:T(8,128)(2,1)}) %reduce-scatter.11.cloned.1.call-update) | async-done | bytes 360464 | tf_op jit(solution)/shard_map/reduce_scatter | solution.py:278
  722.2 1.9 bitcast_convert_fusion.2
  724.1 104.7 %reduce-scatter.5.cloned.1.call-done = bf16[64,4096]{1,0:T(8,128)(2,1)} async-done(((bf16[1024,4096]{1,0:T(8,128)(2,1)}), bf16[64,4096]{1,0:T(8,128)(2,1)}) %reduce-scatter.5.cloned.1.call-update) | async-done | bytes 524304 | tf_op jit(solution)/shard_map/reduce_scatter | solution.py:278
  828.8 2.1 bitcast_convert_fusion.1
  830.9 128.7 %reduce-scatter.9.cloned.1.call-done = bf16[64,5632]{1,0:T(8,128)(2,1)} async-done(((bf16[1024,5632]{1,0:T(8,128)(2,1)}), bf16[64,5632]{1,0:T(8,128)(2,1)}) %reduce-scatter.9.cloned.1.call-update) | async-done | bytes 720912 | tf_op jit(solution)/shard_map/reduce_scatter | solution.py:278
  959.6 2.3 bitcast_convert_fusion
  (369 shorter events, 91.6 us)
Async XLA Ops:
  7.2 3.1 copy-start
  7.2 3.0 copy-start.70
  7.2 3.1 copy-start.55
  7.2 3.3 copy-start.56
  7.2 3.7 copy-start.69
  7.2 80.1 %all-gather.9.cloned.1.call-start = ((), (), s32[]{:S(2)}) async-start(), calls=%async_computation.9 | async-start | bytes 8912896 | tf_op jit(solution)/shard_map/all_gather | solution.py:356
  8.0 121.8 %all-gather.11.cloned.1.call-start = ((), (), s32[]{:S(2)}) async-start(), calls=%async_computation.10 | async-start | bytes 2228224 | tf_op jit(solution)/shard_map/all_gather | solution.py:356
  8.7 215.9 %all-gather.13.cloned.1.call-start = ((), (), s32[]{:S(2)}) async-start(), calls=%async_computation.11 | async-start | bytes 12255232 | tf_op jit(solution)/shard_map/all_gather | solution.py:356
  9.5 274.2 %all-gather.15.cloned.1.call-start = ((), (), s32[]{:S(2)}) async-start(), calls=%async_computation.12 | async-start | bytes 6127616 | tf_op jit(solution)/shard_map/all_gather | solution.py:356
  10.0 4.5 copy-start.59
  10.1 4.5 copy-start.52
  10.1 560.2 %all-reduce.38.cloned.1.call-start = ((), (), s32[]{:S(2)}) async-start(), calls=%async_computation.8 | async-start | bytes 253952 | tf_op jit(solution)/shard_map/psum | solution.py:323
  11.0 81.0 %copy-start.54 = (f32[128,8]{0,1:T(8,128)}, f32[128,8]{0,1:T(8,128)S(1)}, u32[]{:S(2)}) copy-start(f32[128,8]{0,1:T(8,128)S(1)} %copy.138) | copy-start | bytes 12292
  11.3 80.7 %copy-start.37 = (s32[128,1]{1,0:T(8,128)}, s32[128,1]{1,0:T(8,128)S(1)}, u32[]{:S(2)}) copy-start(s32[128,1]{1,0:T(8,128)S(1)} %broadcast_in_dim.182.scol_ref) | copy-start | bytes 1540
  14.6 296.1 %copy-start.57 = (pred[128]{0:T(512)(128)(4,1)}, pred[128]{0:T(512)(128)(4,1)S(1)}, u32[]{:S(2)}) copy-start(pred[128]{0:T(512)(128)(4,1)S(1)} %pad_add_fusion) | copy-start | bytes 388
  289.2 9.3 collective-permute-start
  308.5 7.1 copy-start.53
  337.9 2.9 copy-start.18
  338.5 3.2 copy-start.24
  338.6 3.2 copy-start.5
  338.6 3.2 copy-start.8
  341.8 6.9 slice-start.8
  342.3 6.4 slice-start.9
  342.4 6.4 copy-start.31
  342.4 9.3 slice-start
  342.4 9.5 slice-start.1
  348.7 2.9 copy-start.40
  348.7 4.6 slice-start.2
  401.7 20.0 %slice-start.3 = ((s8[11534336]{0:T(1024)(128)(4,1)}), s8[4194304]{0:T(1024)(128)(4,1)S(1)}, s32[]{:S(2)}) async-start(s8[11534336]{0:T(1024)(128)(4,1)} %bitcast.308), calls=%async_computation.16 | async-start | bytes 8388608
  401.7 20.0 %slice-start.4 = ((s8[11534336]{0:T(1024)(128)(4,1)}), s8[4194304]{0:T(1024)(128)(4,1)S(1)}, s32[]{:S(2)}) async-start(s8[11534336]{0:T(1024)(128)(4,1)} %bitcast.308), calls=%async_computation.17 | async-start | bytes 8388608
  404.6 10.9 %copy-start.32 = (f32[128,1024]{1,0:T(8,128)S(1)}, f32[128,1024]{1,0:T(8,128)}, u32[]{:S(2)}) copy-start(f32[128,1024]{1,0:T(8,128)} %param.14) | copy-start | bytes 1572868
  404.9 10.7 %copy-start.41 = (f32[128,5632]{1,0:T(8,128)S(1)}, f32[128,5632]{1,0:T(8,128)}, u32[]{:S(2)}) copy-start(f32[128,5632]{1,0:T(8,128)} %copy-done.40) | copy-start | bytes 8650756
  405.8 9.7 %collective-permute-start.1 = (bf16[128,1024]{1,0:T(8,128)(2,1)S(1)}, bf16[128,1024]{1,0:T(8,128)(2,1)S(1)}, u32[]{:S(2)}, u32[]{:S(2)}) collective-permute-start(bf16[128,1024]{1,0:T(8,128)(2,1)S(1)} %fusion.70), channel_id=1, source_target_pairs={{16,0},{17,1},{18,2},{19,3},{20,4},{21,5},{22,6},{23,7},{24,8},{25... | collective-permute-start | bytes 786440 | tf_op jit(solution)/shard_map/ppermute | solution.py:23
  415.5 6.1 copy-start.49
  415.6 6.0 copy-start.47
  415.6 6.1 slice-start.5
  421.7 6.4 copy-start.68
  461.0 4.0 copy-start.62
  464.9 3.0 copy-start.2
  467.9 3.0 copy-start.60
  467.9 4.6 copy-start.71
  469.4 3.7 copy-start.3
  476.0 6.9 copy-start.14
  476.0 6.9 copy-start.7
  484.8 153.1 %reduce-scatter.7.cloned.1.call-start = ((), (), s32[]{:S(2)}) async-start(), calls=%async_computation.5 | async-start | bytes 2228224 | tf_op jit(solution)/shard_map/reduce_scatter | solution.py:278
  486.9 235.3 %reduce-scatter.11.cloned.1.call-start = ((), (), s32[]{:S(2)}) async-start(), calls=%async_computation.7 | async-start | bytes 6127616 | tf_op jit(solution)/shard_map/reduce_scatter | solution.py:278
  492.3 336.5 %reduce-scatter.5.cloned.1.call-start = ((), (), s32[]{:S(2)}) async-start(), calls=%async_computation.4 | async-start | bytes 8912896 | tf_op jit(solution)/shard_map/reduce_scatter | solution.py:278
  500.4 459.2 %reduce-scatter.9.cloned.1.call-start = ((), (), s32[]{:S(2)}) async-start(), calls=%async_computation.6 | async-start | bytes 12255232 | tf_op jit(solution)/shard_map/reduce_scatter | solution.py:278
  (45 other events, 74.6 us)
Sparse Core Ops, SparseCore 0:
  10.2 77.0 all-gather.8
  89.5 40.2 all-gather.10
  132.1 92.5 all-gather.12
  226.7 56.8 all-gather.14
  484.9 85.3 all-reduce.37
  573.9 63.9 reduce-scatter.6
  641.8 80.3 reduce-scatter.10
  726.2 102.4 reduce-scatter.4
  832.9 126.6 reduce-scatter.8

commit v2 on v1

--- a/solution.py
+++ b/solution.py
@@ -273,9 +273,38 @@
     return (result, (normed_a, core_back, mixer, middle, normed_f, upgate, hidden))
 
 
-def summed_rows(left, right):
-    part = dot_cols(left, right).astype(jnp.bfloat16)
-    return lax.psum_scatter(part, "dp", scatter_dimension=0, tiled=True).astype(jnp.float32)
+def core_groups():
+    count = lax.axis_size("dp")
+    return [list(range(core, count, 2)) for core in range(2)]
+
+
+def swapped(value):
+    return lax.ppermute(value, "dp", [(i, i ^ 1) for i in range(lax.axis_size("dp"))])
+
+
+def gathered_rows(weight):
+    own = lax.all_gather(weight, "dp", axis=0, axis_index_groups=core_groups())
+    other = swapped(own)
+    even = lax.rem(lax.axis_index("dp"), 2) == 0
+    both = jnp.stack([jnp.where(even, own, other), jnp.where(even, other, own)], axis=1)
+    return both.reshape(-1, weight.shape[1])
+
+
+def paired_part(left, right):
+    rows, width = left.shape
+    count = lax.axis_size("dp")
+    halves = left.reshape(rows, count // 2, 2, width // count)
+    even = lax.rem(lax.axis_index("dp"), 2) == 0
+    first, second = [halves[:, :, i].reshape(rows, width // 2) for i in range(2)]
+    theirs = dot_cols(jnp.where(even, second, first), right).astype(jnp.bfloat16)
+    mine = dot_cols(jnp.where(even, first, second), right)
+    return (mine + swapped(theirs).astype(jnp.float32)).astype(jnp.bfloat16)
+
+
+def summed_rows(part):
+    return lax.psum_scatter(
+        part, "dp", scatter_dimension=0, axis_index_groups=core_groups(), tiled=True
+    ).astype(jnp.float32)
 
 
 def layer_backward(weights, small_params, block, saved, grad_out, sums):
@@ -291,6 +320,11 @@
     d_middle, gain_f = norm_back_f(d_normed_f)
     d_middle = d_middle + grad_out
     dm_bf = d_middle.astype(jnp.bfloat16)
+    if sums:
+        part_up = paired_part(normed_f, d_upgate)
+        part_down = paired_part(g_bf, hidden)
+        dm_bf, part_up, part_down = lax.optimization_barrier((dm_bf, part_up, part_down))
+        sum_up, sum_down = summed_rows(part_up), summed_rows(part_down)
     d_mixer = dot_rows(dm_bf, w_out)
     d_proj, d_gate_pre, d_kernel, d_log, d_bias, d_gain = core_back(d_mixer)
     d_proj = d_proj.astype(jnp.bfloat16)
@@ -302,10 +336,10 @@
     if not sums:
         return d_block
     big = (
-        summed_rows(normed_a, d_proj),
-        summed_rows(mixer, dm_bf),
-        summed_rows(normed_f, d_upgate),
-        summed_rows(g_bf, hidden),
+        summed_rows(paired_part(normed_a, d_proj)),
+        summed_rows(paired_part(mixer, dm_bf)),
+        sum_up,
+        sum_down,
     )
     small = (
         dot_cols(normed_a, d_gate_pre),
@@ -320,7 +354,15 @@
 
 def summed_small(parts):
     flat = jnp.concatenate([part.reshape(-1) for part in parts])
-    flat = lax.psum(flat, "dp")
+    count = lax.axis_size("dp")
+    if count & (count - 1):
+        flat = lax.psum(flat, "dp")
+    else:
+        step = 1
+        while step < count:
+            pairs = [(i, i ^ step) for i in range(count)]
+            flat = flat + lax.ppermute(flat, "dp", pairs)
+            step *= 2
     outs, start = [], 0
     for part in parts:
         outs.append(flat[start : start + part.size].reshape(part.shape))
@@ -352,9 +394,7 @@
         decay_bias[0],
         out_gain[0],
     )
-    weights = tuple(
-        lax.all_gather(weight[0], "dp", axis=0, tiled=True) for weight in (w_in, w_out, w_up, w_down)
-    )
+    weights = tuple(gathered_rows(weight[0]) for weight in (w_in, w_out, w_up, w_down))
     segment = segment_ids(marks)
     early_out, _ = layer_forward(weights, small_params, block_input, segment)
     arrived = passed_along(early_out.astype(jnp.bfloat16), "section", 1).astype(jnp.float32)

time: 975 us -> 902 us (0.925)
  waiting for transfers between devices: 675 us -> 543 us
  other arithmetic: 78 us -> 117 us
  matrix products: 93 us -> 106 us
    reduce_scatter x4, waiting for transfers between devices: 377 us -> 237 us  [summed_rows(): lax.psum_scatter(part, 'dp', scatter_dimension=0, axis_index_groups=core_...]
    psum x1 -> x0, waiting for transfers between devices: 53.2 us -> none  [summed_small(): flat = lax.psum(flat, 'dp')]
    another operation x1 -> x9, other arithmetic: 0.03 us -> 37.1 us  [the longest x8 37.1 us: gathered_rows(): jnp.stack([jnp.where(even, own, other), jnp.where(even, other, own)], axi...]
    ppermute x0 -> x12, waiting for transfers between devices: none -> 36.4 us  [the longest x4 26.7 us: summed_small(): flat = flat + lax.ppermute(flat, 'dp', pairs)]
    all_gather x4, waiting for transfers between devices: 230 us -> 254 us  [gathered_rows(): own = lax.all_gather(weight, 'dp', axis=0, axis_index_groups=core_groups())]
    reshape x0 -> x6, local copies, waits for them, and re-layouts: none -> 11.3 us  [the longest x3 6.17 us: mixer_core(): gate_part = proj[:, 3 * D:].reshape(heads_shape)]
    dot_general x5 -> x9, matrix products: 21 us -> 29.7 us  [dot_cols(): lax.dot_general(left, right, (((0,), (0,)), ((), ())), preferred_element_...]
    unnamed x180 -> x223, local copies, waits for them, and re-layouts: 23.3 us -> 20.1 us
  transfers between devices with their start and end apart: 11 -> 22, of which waited for: 11 -> 15; matrix products, arithmetic and copies ran while one was open for 7% -> 14% of each run, Pallas kernels for 1% -> 3%
where the time goes in v2:
time: 902 us; the launch traced here: 897 us
  waiting for transfers between devices  543 us (60%)
  other arithmetic  117 us (13%)
  matrix products  106 us (12%)
  Pallas kernels  54.7 us (6%)
  local copies, waits for them, and re-layouts  53.4 us (6%)
  between operations  16 us (2%)
    all_gather x4, waiting for transfers between devices, gathered_rows(): own = lax.all_gather(weight, 'dp', axis=0, axis_index_groups=core_groups())  254 us
    reduce_scatter x4, waiting for transfers between devices, summed_rows(): lax.psum_scatter(part, 'dp', scatter_dimension=0, axis_index_groups=core_...  237 us
    dot_general x10, matrix products, dot_rows(): lax.dot_general(left, right, (((1,), (1,)), ((), ())), preferred_element_...  44.4 us
    another operation x8, other arithmetic, gathered_rows(): jnp.stack([jnp.where(even, own, other), jnp.where(even, other, own)], axi...  37.1 us
    dot_general x9, matrix products, dot_cols(): lax.dot_general(left, right, (((0,), (0,)), ((), ())), preferred_element_...  29.7 us
    pallas_call x2, Pallas kernels, delta_call(): pl.pallas_call(kernel, grid=(rows // BLOCK, HEADS // GROUP_HEADS), in_spe...  27.4 us
    pallas_call x2, Pallas kernels, delta_rule(): delta_core(wide(queries), wide(key_rows), wide(value_rows), beta_rows, cu...  27.3 us
    ppermute x4, waiting for transfers between devices, summed_small(): flat = flat + lax.ppermute(flat, 'dp', pairs)  26.7 us
  transfers between devices with their start and end apart: 22, of which 15 were waited for; matrix products, arithmetic and copies ran while one was open for 14% of the time, Pallas kernels for 3%

profile of v2, /device:TPU:0, one launch (start us, length us, event | category | flops | bytes accessed | tf_op | source)
XLA Modules:
  0.0 897.4 jit_solution(1846095711657750756)
XLA Ops:
  10.7 59.6 %all-gather.11.cloned.1.call-done = bf16[8,64,2816]{2,1,0:T(8,128)(2,1)} async-done(((bf16[1,64,2816]{2,1,0:T(8,128)(2,1)}), bf16[8,64,2816]{2,1,0:T(8,128)(2,1)}) %all-gather.11.cloned.1.call-update) | async-done | bytes 2883600 | tf_op jit(solution)/shard_map/all_gather | solution.py:286
  70.4 73.4 %all-gather.5.cloned.1.call-done = bf16[8,64,4096]{2,1,0:T(8,128)(2,1)} async-done(((bf16[1,64,4096]{2,1,0:T(8,128)(2,1)}), bf16[8,64,4096]{2,1,0:T(8,128)(2,1)}) %all-gather.5.cloned.1.call-update) | async-done | bytes 4194320 | tf_op jit(solution)/shard_map/all_gather | solution.py:286
  144.3 40.6 %all-gather.7.cloned.1.call-done = bf16[8,64,1024]{2,1,0:T(8,128)(2,1)} async-done(((bf16[1,64,1024]{2,1,0:T(8,128)(2,1)}), bf16[8,64,1024]{2,1,0:T(8,128)(2,1)}) %all-gather.7.cloned.1.call-update) | async-done | bytes 1048592 | tf_op jit(solution)/shard_map/all_gather | solution.py:286
  194.0 4.0 select_bitcast_fusion.5
  198.0 80.0 %all-gather.9.cloned.1.call-done = bf16[8,64,5632]{2,1,0:T(8,128)(2,1)} async-done(((bf16[1,64,5632]{2,1,0:T(8,128)(2,1)}), bf16[8,64,5632]{2,1,0:T(8,128)(2,1)}) %all-gather.9.cloned.1.call-update) | async-done | bytes 5767184 | tf_op jit(solution)/shard_map/all_gather | solution.py:286
  277.9 5.0 pad_maximum_fusion.2
  282.9 4.2 select_bitcast_fusion.3
  287.1 6.2 pad_maximum_fusion.1
  293.3 4.7 fusion.83
  304.1 2.7 fusion.94
  306.8 13.6 %jvp__.2 = (f32[128,1024]{1,0:T(8,128)}, f32[128,1024]{1,0:T(8,128)}, f32[128,1024]{1,0:T(8,128)}) custom-call(f32[128,1024]{1,0:T(8,128)} %get-tuple-element.161.q_ref, f32[128,1024]{1,0:T(8,128)} %get-tuple-element.162.k_ref, f32[128,1024]{1,0:T(8,128)} %get-tuple-element.160.v_ref, f32[8,128,1]{2,1,0:T(8,128)} %copy.273.beta_ref, ...), custom_call_target="tpu_custom_call" | custom-call | flops 3355443200 | bytes 5242880 | tf_op jit(solution)/shard_map/jvp()/pallas_call | solution.py:168
  324.6 9.5 %select_bitcast_fusion.1 = (bf16[8,1,64,5632]{3,2,1,0:T(8,128)(2,1)}, bf16[8,1,64,5632]{3,2,1,0:T(8,128)(2,1)}) fusion(bf16[8,64,5632]{2,1,0:T(8,128)(2,1)} %all-gather.9.cloned.1.call-done, bf16[8,64,5632]{2,1,0:T(8,128)(2,1)} %collective-permute-done.2, pred[]{:T(512)S(6)} %eq.46), kind=kLoop, calls=%fused_computation.9 | loop fusion | flops 5767168 | bytes 23068672 | tf_op jit(solution)/shard_map/stack | solution.py:289
  334.1 6.7 pad_maximum_fusion
  342.6 2.5 copy-done.1
  347.1 3.4 collective-permute-start.4
  352.3 4.4 collective-permute-done.4
  357.8 4.6 fusion.97
  364.2 2.7 fusion.11
  373.8 2.8 fusion.93
  376.6 13.8 %jvp__.3 = (f32[128,1024]{1,0:T(8,128)}, f32[128,1024]{1,0:T(8,128)}, f32[128,1024]{1,0:T(8,128)}) custom-call(f32[128,1024]{1,0:T(8,128)} %get-tuple-element.156.q_ref, f32[128,1024]{1,0:T(8,128)} %get-tuple-element.157.k_ref, f32[128,1024]{1,0:T(8,128)} %get-tuple-element.155.v_ref, f32[8,128,1]{2,1,0:T(8,128)} %copy.286.beta_ref, ...), custom_call_target="tpu_custom_call" | custom-call | flops 3355443200 | bytes 5242880 | tf_op jit(solution)/shard_map/jvp()/pallas_call | solution.py:168
  399.2 6.1 fusion.98
  405.4 3.0 fusion.88
  409.6 6.4 multiply_reduce_fusion.12
  426.0 13.7 %transpose_jvp___.2 = (f32[128,1024]{1,0:T(8,128)}, f32[128,1024]{1,0:T(8,128)}, f32[128,1024]{1,0:T(8,128)}, f32[8,128,1]{2,1,0:T(8,128)}, f32[8,128,1]{2,1,0:T(8,128)}, /*index=5*/f32[8,1,128]{2,1,0:T(1,128)}) custom-call(f32[128,1024]{1,0:T(8,128)} %get-tuple-element.156.q_ref, f32[128,1024]{1,0:T(8,128)} %get-tuple-element.157.k_ref, ...), custom_call_target="tpu_custom_call" | custom-call | flops 2013265920 | bytes 5242880 | tf_op jit(solution)/shard_map/transpose(jvp())/pallas_call | solution.py:219
  448.1 3.0 add_add_fusion.7
  463.5 3.4 multiply_add_fusion.2
  466.9 6.4 multiply_reduce_fusion.10
  477.4 7.6 collective-permute-done.5
  486.7 6.7 fusion.87
  496.8 6.1 convolution_convert_fusion
  503.0 2.4 convolution_convert_fusion.2
  508.7 9.7 %multiply_reduce_fusion.5 = (f32[1024]{0:T(1024)}, f32[128]{0:T(128)S(1)}, f32[128,1024]{1,0:T(8,128)S(1)}) fusion(f32[128,1024]{1,0:T(8,128)S(1)} %get-tuple-element.194, f32[128]{0:T(128)S(1)} %copy-done.59, f32[1024]{0:T(1024)S(1)} %bitcast.355, bf16[1024,5632]{1,0:T(8,128)(2,1)} %bitcast.283, f32[128,2816]{1,0:T(8,128)} %get-tuple-element.140, ...), kind=kOutput, calls=%fused_computation.115 | convolution fusion | flops 1478622080 | bytes 15475712 | tf_op jit(solution)/shard_map/dot_general | solution.py:27
  520.4 4.3 add_convert_fusion.2
  524.7 7.7 add_convert_fusion
  533.8 2.6 collective-permute-done.9
  540.3 4.3 multiply_reduce_fusion.4
  547.7 13.6 %transpose_jvp___.3 = (f32[128,1024]{1,0:T(8,128)}, f32[128,1024]{1,0:T(8,128)}, f32[128,1024]{1,0:T(8,128)}, f32[8,128,1]{2,1,0:T(8,128)}, f32[8,128,1]{2,1,0:T(8,128)}, /*index=5*/f32[8,1,128]{2,1,0:T(1,128)}) custom-call(f32[128,1024]{1,0:T(8,128)} %get-tuple-element.156.q_ref, f32[128,1024]{1,0:T(8,128)} %get-tuple-element.157.k_ref, ...), custom_call_target="tpu_custom_call" | custom-call | flops 2013265920 | bytes 5242880 | tf_op jit(solution)/shard_map/transpose(jvp())/pallas_call | solution.py:219
  565.1 3.0 add_add_fusion.2
  574.8 4.7 multiply_reduce_fusion.3
  582.7 7.1 collective-permute-done.8
  589.8 3.3 add_convert_fusion.1
  599.9 7.3 multiply_reduce_fusion.6
  609.5 5.7 fusion.15
  617.4 11.2 %collective-permute-done.12 = f32[30864]{0:T(1024)S(1)} collective-permute-done((f32[30864]{0:T(1024)S(1)}, f32[30864]{0:T(1024)S(1)}, u32[]{:S(2)}, u32[]{:S(2)}) %collective-permute-start.12) | collective-permute-done | bytes 123488 | tf_op jit(solution)/shard_map/ppermute | solution.py:364
  629.6 12.2 %collective-permute-done.13 = f32[30864]{0:T(1024)S(1)} collective-permute-done((f32[30864]{0:T(1024)S(1)}, f32[30864]{0:T(1024)S(1)}, u32[]{:S(2)}, u32[]{:S(2)}) %collective-permute-start.13) | collective-permute-done | bytes 123488 | tf_op jit(solution)/shard_map/ppermute | solution.py:364
  646.9 36.4 %reduce-scatter.11.cloned.1.call-done = bf16[64,2816]{1,0:T(8,128)(2,1)} async-done(((bf16[512,2816]{1,0:T(8,128)(2,1)}), bf16[64,2816]{1,0:T(8,128)(2,1)}) %reduce-scatter.11.cloned.1.call-update) | async-done | bytes 360464 | tf_op jit(solution)/shard_map/reduce_scatter | solution.py:305
  685.2 111.6 %reduce-scatter.9.cloned.1.call-done = bf16[64,5632]{1,0:T(8,128)(2,1)} async-done(((bf16[512,5632]{1,0:T(8,128)(2,1)}), bf16[64,5632]{1,0:T(8,128)(2,1)}) %reduce-scatter.9.cloned.1.call-update) | async-done | bytes 720912 | tf_op jit(solution)/shard_map/reduce_scatter | solution.py:305
  799.2 89.0 %reduce-scatter.5.cloned.1.call-done = bf16[64,4096]{1,0:T(8,128)(2,1)} async-done(((bf16[512,4096]{1,0:T(8,128)(2,1)}), bf16[64,4096]{1,0:T(8,128)(2,1)}) %reduce-scatter.5.cloned.1.call-update) | async-done | bytes 524304 | tf_op jit(solution)/shard_map/reduce_scatter | solution.py:305
  (450 shorter events, 138.6 us)
Async XLA Ops:
  7.2 136.8 %copy-start = (bf16[1,1024,16]{1,2,0:T(8,128)(2,1)S(1)}, bf16[1,1024,16]{1,2,0:T(8,128)(2,1)}, u32[]{:S(2)}) copy-start(bf16[1,1024,16]{1,2,0:T(8,128)(2,1)} %param.20) | copy-start | bytes 98308
  7.2 63.1 %copy-start.15 = (f32[128,1024]{1,0:T(8,128)S(1)}, f32[128,1024]{1,0:T(8,128)}, u32[]{:S(2)}) copy-start(f32[128,1024]{1,0:T(8,128)} %param.13) | copy-start | bytes 1572868
  7.2 136.7 %copy-start.96 = (f32[1,8]{1,0:T(1,128)S(1)}, f32[1,8]{1,0:T(1,128)}, u32[]{:S(2)}) copy-start(f32[1,8]{1,0:T(1,128)} %param.23) | copy-start | bytes 100
  7.2 136.7 %copy-start.60 = (f32[1,2,1024]{2,1,0:T(2,128)S(1)}, f32[1,2,1024]{2,1,0:T(2,128)}, u32[]{:S(2)}) copy-start(f32[1,2,1024]{2,1,0:T(2,128)} %param.21) | copy-start | bytes 24580
  7.2 137.0 %copy-start.61 = (f32[1,8]{1,0:T(1,128)S(1)}, f32[1,8]{1,0:T(1,128)}, u32[]{:S(2)}) copy-start(f32[1,8]{1,0:T(1,128)} %param.24) | copy-start | bytes 100
  7.2 63.1 %all-gather.11.cloned.1.call-start = ((), (), s32[]{:S(2)}) async-start(), calls=%async_computation.7 | async-start | bytes 3244032 | tf_op jit(solution)/shard_map/all_gather | solution.py:286
  8.0 135.9 %all-gather.5.cloned.1.call-start = ((), (), s32[]{:S(2)}) async-start(), calls=%async_computation.4 | async-start | bytes 4718592 | tf_op jit(solution)/shard_map/all_gather | solution.py:286
  8.7 176.1 %all-gather.7.cloned.1.call-start = ((), (), s32[]{:S(2)}) async-start(), calls=%async_computation.5 | async-start | bytes 1179648 | tf_op jit(solution)/shard_map/all_gather | solution.py:286
  9.5 268.5 %all-gather.9.cloned.1.call-start = ((), (), s32[]{:S(2)}) async-start(), calls=%async_computation.6 | async-start | bytes 6488064 | tf_op jit(solution)/shard_map/all_gather | solution.py:286
  10.0 635.3 %reduce-scatter.7.cloned.1.call-start = ((), (), s32[]{:S(2)}) async-start(), calls=%async_computation.9 | async-start | bytes 1179648 | tf_op jit(solution)/shard_map/reduce_scatter | solution.py:305
  10.1 179.7 %copy-start.80 = (f32[1,128]{1,0:T(1,128)S(1)}, f32[1,128]{1,0:T(1,128)}, u32[]{:S(2)}) copy-start(f32[1,128]{1,0:T(1,128)} %param.25) | copy-start | bytes 1540
  10.1 180.3 %copy-start.52 = (f32[1,4,3072]{2,1,0:T(4,128)S(1)}, f32[1,4,3072]{2,1,0:T(4,128)}, u32[]{:S(2)}) copy-start(f32[1,4,3072]{2,1,0:T(4,128)} %param.22) | copy-start | bytes 147460
  10.4 180.8 %copy-start.29 = (s32[128,1]{1,0:T(8,128)}, s32[128,1]{1,0:T(8,128)S(1)}, u32[]{:S(2)}) copy-start(s32[128,1]{1,0:T(8,128)S(1)} %broadcast_in_dim.178.scol_ref) | copy-start | bytes 1540
  10.5 177.3 %copy-start.90 = (pred[126]{0:T(512)(128)(4,1)}, pred[126]{0:T(512)(128)(4,1)S(1)}, u32[]{:S(2)}) copy-start(pred[126]{0:T(512)(128)(4,1)S(1)} %fusion.46) | copy-start | bytes 382
  10.7 177.2 %copy-start.88 = (pred[125]{0:T(512)(128)(4,1)}, pred[125]{0:T(512)(128)(4,1)S(1)}, u32[]{:S(2)}) copy-start(pred[125]{0:T(512)(128)(4,1)S(1)} %fusion.47) | copy-start | bytes 379
  70.3 122.5 %collective-permute-start.3 = (bf16[8,64,2816]{2,1,0:T(8,128)(2,1)}, bf16[8,64,2816]{2,1,0:T(8,128)(2,1)}, u32[]{:S(2)}, u32[]{:S(2)}) collective-permute-start(bf16[8,64,2816]{2,1,0:T(8,128)(2,1)} %all-gather.11.cloned.1.call-done), channel_id=1, source_target_pairs={{0,1},{1,0},{2,3},{3,2},{4,5},{5,4},{6,7},{7,6},{8,9},{9,8},{10,11... | collective-permute-start | bytes 8650760 | tf_op jit(solution)/shard_map/ppermute | solution.py:282
  143.9 139.1 %collective-permute-start = (bf16[8,64,4096]{2,1,0:T(8,128)(2,1)}, bf16[8,64,4096]{2,1,0:T(8,128)(2,1)}, u32[]{:S(2)}, u32[]{:S(2)}) collective-permute-start(bf16[8,64,4096]{2,1,0:T(8,128)(2,1)} %all-gather.5.cloned.1.call-done), channel_id=1, source_target_pairs={{0,1},{1,0},{2,3},{3,2},{4,5},{5,4},{6,7},{7,6},{8,9},{9,8},{10,11... | collective-permute-start | bytes 12582920 | tf_op jit(solution)/shard_map/ppermute | solution.py:282
  143.9 43.9 %copy-start.78 = (f32[128]{0:T(128)}, f32[128]{0:T(128)S(1)}, u32[]{:S(2)}) copy-start(f32[128]{0:T(128)S(1)} %add_rsqrt_fusion.6) | copy-start | bytes 1540
  143.9 43.9 %copy-start.65 = (f32[8]{0:T(128)}, f32[8]{0:T(128)S(1)}, u32[]{:S(2)}) copy-start(f32[8]{0:T(128)S(1)} %negate_bitcast_fusion) | copy-start | bytes 100
  184.8 6.2 collective-permute-start.1
  277.9 46.7 %collective-permute-start.2 = (bf16[8,64,5632]{2,1,0:T(8,128)(2,1)}, bf16[8,64,5632]{2,1,0:T(8,128)(2,1)}, u32[]{:S(2)}, u32[]{:S(2)}) collective-permute-start(bf16[8,64,5632]{2,1,0:T(8,128)(2,1)} %all-gather.9.cloned.1.call-done), channel_id=1, source_target_pairs={{0,1},{1,0},{2,3},{3,2},{4,5},{5,4},{6,7},{7,6},{8,9},{9,8},{10,11... | collective-permute-start | bytes 17301512 | tf_op jit(solution)/shard_map/ppermute | solution.py:282
  324.6 20.4 %slice-start.3 = ((s8[5767168]{0:T(1024)(128)(4,1)}), s8[1572864]{0:T(1024)(128)(4,1)S(1)}, s32[]{:S(2)}) async-start(s8[5767168]{0:T(1024)(128)(4,1)} %bitcast.293), calls=%async_computation.15 | async-start | bytes 3145728
  334.1 10.9 %slice-start.4 = ((s8[5767168]{0:T(1024)(128)(4,1)}), s8[4194304]{0:T(1024)(128)(4,1)S(1)}, s32[]{:S(2)}) async-start(s8[5767168]{0:T(1024)(128)(4,1)} %bitcast.293), calls=%async_computation.16 | async-start | bytes 8388608
  347.1 9.6 %collective-permute-start.4 = (bf16[128,1024]{1,0:T(8,128)(2,1)S(1)}, bf16[128,1024]{1,0:T(8,128)(2,1)S(1)}, u32[]{:S(2)}, u32[]{:S(2)}) collective-permute-start(bf16[128,1024]{1,0:T(8,128)(2,1)S(1)} %fusion.16), channel_id=1, source_target_pairs={{0,16},{1,17},{2,18},{3,19},{4,20},{5,21},{6,22},{7,23},{8,24},{9,... | collective-permute-start | bytes 786440 | tf_op jit(solution)/shard_map/ppermute | solution.py:23
  396.1 9.3 %slice-start.5 = ((s8[5767168]{0:T(1024)(128)(4,1)}), s8[4194304]{0:T(1024)(128)(4,1)S(1)}, s32[]{:S(2)}) async-start(s8[5767168]{0:T(1024)(128)(4,1)} %bitcast.296), calls=%async_computation.17 | async-start | bytes 8388608
  398.4 20.3 %copy-start.58 = (f32[128]{0:T(128)}, f32[128]{0:T(128)S(1)}, u32[]{:S(2)}) copy-start(f32[128]{0:T(128)S(1)} %fusion.74) | copy-start | bytes 1540
  399.2 9.2 %slice-start = ((s8[11534336]{0:T(1024)(128)(4,1)}), s8[4194304]{0:T(1024)(128)(4,1)S(1)}, s32[]{:S(2)}) async-start(s8[11534336]{0:T(1024)(128)(4,1)} %bitcast.284), calls=%async_computation.12 | async-start | bytes 8388608
  399.2 9.2 %slice-start.1 = ((s8[11534336]{0:T(1024)(128)(4,1)}), s8[4194304]{0:T(1024)(128)(4,1)S(1)}, s32[]{:S(2)}) async-start(s8[11534336]{0:T(1024)(128)(4,1)} %bitcast.284), calls=%async_computation.13 | async-start | bytes 8388608
  474.8 10.2 %collective-permute-start.5 = (bf16[128,1024]{1,0:T(8,128)(2,1)}, bf16[128,1024]{1,0:T(8,128)(2,1)}, u32[]{:S(2)}, u32[]{:S(2)}) collective-permute-start(bf16[128,1024]{1,0:T(8,128)(2,1)} %fusion.21), channel_id=1, source_target_pairs={{16,0},{17,1},{18,2},{19,3},{20,4},{21,5},{22,6},{23,7},{24,8},{25... | collective-permute-start | bytes 786440 | tf_op jit(solution)/shard_map/ppermute | solution.py:23
  486.7 8.5 copy-start.43
  502.9 21.7 %collective-permute-start.6 = (bf16[512,5632]{1,0:T(8,128)(2,1)}, bf16[512,5632]{1,0:T(8,128)(2,1)}, u32[]{:S(2)}, u32[]{:S(2)}) collective-permute-start(bf16[512,5632]{1,0:T(8,128)(2,1)} %convolution_convert_fusion), channel_id=1, source_target_pairs={{0,1},{1,0},{2,3},{3,2},{4,5},{5,4},{6,7},{7,6},{8,9},{9,8},{10,11... | collective-permute-start | bytes 17301512 | tf_op jit(solution)/shard_map/ppermute | solution.py:282
  505.4 15.0 %collective-permute-start.7 = (bf16[512,2816]{1,0:T(8,128)(2,1)}, bf16[512,2816]{1,0:T(8,128)(2,1)}, u32[]{:S(2)}, u32[]{:S(2)}) collective-permute-start(bf16[512,2816]{1,0:T(8,128)(2,1)} %convolution_convert_fusion.2), channel_id=1, source_target_pairs={{0,1},{1,0},{2,3},{3,2},{4,5},{5,4},{6,7},{7,6},{8,9},{9,8},{10,11... | collective-permute-start | bytes 8650760 | tf_op jit(solution)/shard_map/ppermute | solution.py:282
  508.7 9.7 %copy-start.94 = (f32[128]{0:T(128)S(1)}, f32[128]{0:T(128)}, u32[]{:S(2)}) copy-start(f32[128]{0:T(128)} %get-tuple-element.128) | copy-start | bytes 1540
  508.7 9.7 %copy-start.27 = (f32[128,1024]{1,0:T(8,128)S(1)}, f32[128,1024]{1,0:T(8,128)}, u32[]{:S(2)}) copy-start(f32[128,1024]{1,0:T(8,128)} %param.14) | copy-start | bytes 1572868
  533.7 2.7 collective-permute-start.9
  538.7 144.6 %reduce-scatter.11.cloned.1.call-start = ((), (), s32[]{:S(2)}) async-start(), calls=%async_computation.11 | async-start | bytes 3244032 | tf_op jit(solution)/shard_map/reduce_scatter | solution.py:305
  539.3 257.5 %reduce-scatter.9.cloned.1.call-start = ((), (), s32[]{:S(2)}) async-start(), calls=%async_computation.10 | async-start | bytes 6488064 | tf_op jit(solution)/shard_map/reduce_scatter | solution.py:305
  540.1 348.1 %reduce-scatter.5.cloned.1.call-start = ((), (), s32[]{:S(2)}) async-start(), calls=%async_computation.8 | async-start | bytes 4718592 | tf_op jit(solution)/shard_map/reduce_scatter | solution.py:305
  581.3 8.5 copy-start.47
  582.6 7.2 collective-permute-start.8
  599.9 7.5 copy-start.92
  607.5 1.4 collective-permute-start.10
  608.9 8.5 copy-start.93
  608.9 19.8 %copy-start.39 = (f32[128,1024]{1,0:T(8,128)S(1)}, f32[128,1024]{1,0:T(8,128)}, u32[]{:S(2)}) copy-start(f32[128,1024]{1,0:T(8,128)} %get-tuple-element.203) | copy-start | bytes 1572868
  608.9 19.8 %copy-start.40 = (f32[128,1024]{1,0:T(8,128)S(1)}, f32[128,1024]{1,0:T(8,128)}, u32[]{:S(2)}) copy-start(f32[128,1024]{1,0:T(8,128)} %get-tuple-element.124) | copy-start | bytes 1572868
  608.9 8.4 collective-permute-start.11
  617.3 11.3 %collective-permute-start.12 = (f32[30864]{0:T(1024)S(1)}, f32[30864]{0:T(1024)S(1)}, u32[]{:S(2)}, u32[]{:S(2)}) collective-permute-start(f32[30864]{0:T(1024)S(1)} %add.358), channel_id=1, source_target_pairs={{0,4},{1,5},{2,6},{3,7},{4,0},{5,1},{6,2},{7,3},{8,12},{9,13},{10,... | collective-permute-start | bytes 370376 | tf_op jit(solution)/shard_map/ppermute | solution.py:364
  628.6 13.2 %collective-permute-start.13 = (f32[30864]{0:T(1024)S(1)}, f32[30864]{0:T(1024)S(1)}, u32[]{:S(2)}, u32[]{:S(2)}) collective-permute-start(f32[30864]{0:T(1024)S(1)} %add.359), channel_id=1, source_target_pairs={{0,8},{1,9},{2,10},{3,11},{4,12},{5,13},{6,14},{7,15},{8,0},{9,1},... | collective-permute-start | bytes 370376 | tf_op jit(solution)/shard_map/ppermute | solution.py:364
  (79 other events, 271.0 us)
Sparse Core Ops, SparseCore 0:
  10.2 60.0 all-gather.10
  72.4 71.3 all-gather.4
  146.0 38.7 all-gather.6
  186.9 91.0 all-gather.8
  538.9 61.4 reduce-scatter.6
  603.8 79.5 reduce-scatter.10
  687.0 109.8 reduce-scatter.8
  800.5 87.6 reduce-scatter.4
